TPU v7x, 128 devices: a whole 4x4x4 slice. The times are simulated.
128 devices in a mesh: walk: 16 (over y_hi, z, core), band: 8 (over y_lo, x).
Axes of the slice: x: 4, y: 4 (y_hi: 2, y_lo: 2; y = y_hi * 2 + y_lo), z: 4, core: 2. Of those that a mesh axis runs over, the one named last changes fastest.
Arguments:
- positions: float32 [2, 49152], P(None, 'walk'), may hold values from 0 to 1
- coefficients: bfloat16 [2, 18432, 1024], P(None, 'walk', 'band')
- lattice: int32 [2, 18432], replicated, may hold values from -76 to 76
- spin_labels: int32 [49152], P('walk'), may hold values from 0 to 1
- occupied: int32 [2, 48], replicated, may hold values from 0 to 1023
- features: bfloat16 [49152, 256], P('walk'), may hold values from -6 to 6
- orbital_head: bfloat16 [256, 192], replicated, may hold values from -0.029907227 to 0.029907227
Outputs:
- gradient: float32 [256, 192], replicated
All inputs are finite; a program needn't handle non-finite values.
Results may differ from a plain program's by a relative error of at most 0.0003.
Values may be sent and summed in bfloat16 or wider, within the bound.
No kernel may reach another device: no remote copies, remote signals or barrier semaphores. Data moves between devices by JAX's collectives and lax.ppermute only.
A program may use at most 128 MiB of HBM per device.

v0:
```python
import functools

import jax
import jax.numpy as jnp
from jax import lax
from jax.experimental import pallas as pl
from jax.experimental.pallas import tpu as pltpu
from jax.sharding import PartitionSpec as P


INTERPRET = False
F32 = jnp.float32
BF16 = jnp.bfloat16
PI = 3.141592653589793
BLOCK = 24
RUN = 1024
HALF = 80
LANES = 128


def split3(value):
    high = value.astype(BF16)
    rest = value - high.astype(F32)
    middle = rest.astype(BF16)
    low = (rest - middle.astype(F32)).astype(BF16)
    return high, middle, low


def pick_kernel(coef_hbm, occ_hbm, out_ref, coef_ref, occ_ref, stage_ref, sems):
    copies = [pltpu.make_async_copy(occ_hbm, occ_ref, sems.at[2])]
    copies += [pltpu.make_async_copy(coef_hbm.at[part], coef_ref.at[part], sems.at[part]) for part in range(2)]
    for copy in copies:
        copy.start()
    _, rows, bands = coef_ref.shape
    spins, per_spin = occ_ref.shape
    devices = stage_ref.shape[0] // BLOCK
    senders = lax.axis_size("band")
    each = spins * per_spin // senders
    tiles = rows // LANES
    base = lax.axis_index("band") * bands
    for row in range(2 * tiles, BLOCK):
        stage_ref[pl.ds(row, devices, stride=BLOCK), :] = jnp.zeros((devices, LANES), F32)
    line = lax.broadcasted_iota(jnp.int32, (8, bands), 0)
    lane = lax.broadcasted_iota(jnp.int32, (8, bands), 1) + base
    copies[0].wait()
    picks = []
    for group in range(devices // senders):
        wanted = jnp.full((8, bands), -1, jnp.int32)
        if group < each:
            for sender in range(senders):
                orbital = sender * each + group
                wanted = jnp.where(line == sender, occ_ref[orbital // per_spin, orbital % per_spin], wanted)
        picks.append(jnp.where(lane == wanted, 1.0, 0.0))
    pick = jnp.concatenate(picks, axis=0).astype(BF16)
    for part in range(2):
        copies[1 + part].wait()
        taken = lax.dot_general(
            pick, coef_ref[part], (((1,), (1,)), ((), ())), preferred_element_type=F32
        )
        for tile in range(tiles):
            stage_ref[pl.ds(part * tiles + tile, devices, stride=BLOCK), :] = taken[:, tile * LANES : (tile + 1) * LANES]
    out_ref[...] = stage_ref[...].astype(BF16)


def order_kernel(pos_ref, label_ref, out_ref, slot_ref, up_ref):
    chunks = label_ref.shape[0]
    own = RUN // LANES
    runs = chunks // own
    up = label_ref[...] == 0
    ones = jnp.where(up, 1.0, 0.0)
    row = lax.broadcasted_iota(jnp.int32, (LANES, LANES), 0)
    column = lax.broadcasted_iota(jnp.int32, (LANES, LANES), 1)
    until = jnp.where(row <= column, 1.0, 0.0).astype(BF16)
    inside = jnp.dot(ones.astype(BF16), until, preferred_element_type=F32)
    whole = jnp.broadcast_to(inside[:, LANES - 1 : LANES], inside.shape).astype(BF16)
    row = lax.broadcasted_iota(jnp.int32, (chunks, chunks), 0)
    column = lax.broadcasted_iota(jnp.int32, (chunks, chunks), 1)
    same = jnp.where(row // own == column // own, 1.0, 0.0)
    before = jnp.where(column < row, same, 0.0).astype(BF16)
    rank = inside + jnp.dot(before, whole, preferred_element_type=F32)
    total = jnp.dot(same.astype(BF16), whole, preferred_element_type=F32)
    place = (
        lax.broadcasted_iota(jnp.int32, rank.shape, 0) % own * LANES + lax.broadcasted_iota(jnp.int32, rank.shape, 1)
    ).astype(F32)
    slot = jnp.where(up, rank - 1.0, total + place - rank)
    first = jnp.where(place < total, 1.0, 0.0)
    up_ref[...] = jnp.concatenate([first[chunk : chunk + 1, :] for chunk in range(chunks)], axis=1)
    parts = jnp.concatenate([part.astype(F32) for part in split3(pos_ref[...])], axis=0).astype(BF16)
    here = lax.broadcasted_iota(jnp.int32, (RUN, RUN), 0).astype(F32)
    for run in range(runs):
        line = jnp.concatenate([slot[run * own + k : run * own + k + 1, :] for k in range(own)], axis=1)
        slot_ref[run : run + 1, :] = line
        move = jnp.where(here == line, 1.0, 0.0).astype(BF16)
        moved = lax.dot_general(
            parts[:, run * RUN : (run + 1) * RUN], move, (((1,), (1,)), ((), ())), preferred_element_type=F32
        )
        moved = moved[0:2] + moved[2:4] + moved[4:6]
        for axis in range(2):
            for k in range(own):
                at = axis * chunks + run * own + k
                out_ref[at : at + 1, :] = moved[axis : axis + 1, k * LANES : (k + 1) * LANES]
        out_ref[2 * chunks + run : 2 * chunks + run + 1, :] = total[run * own : run * own + 1, :]
    out_ref[2 * chunks + runs :, :] = jnp.zeros((out_ref.shape[0] - 2 * chunks - runs, LANES), F32)


def sort_kernel(slot_ref, feature_ref, head_ref, up_ref, out_ref, net_ref):
    here = lax.broadcasted_iota(jnp.int32, (RUN, RUN), 0).astype(F32)
    for run in range(slot_ref.shape[0]):
        move = jnp.where(here == slot_ref[run : run + 1, :], 1.0, 0.0).astype(BF16)
        moved = jnp.dot(move, feature_ref[run * RUN : (run + 1) * RUN, :], preferred_element_type=F32).astype(BF16)
        out_ref[run * RUN : (run + 1) * RUN, :] = moved
        net_ref[: head_ref.shape[0], run * RUN : (run + 1) * RUN] = lax.dot_general(
            head_ref[...], moved, (((1,), (1,)), ((), ())), preferred_element_type=F32
        )
    tail = net_ref.shape[0] - head_ref.shape[0]
    net_ref[head_ref.shape[0] :, :] = jnp.broadcast_to(up_ref[...], (tail, up_ref.shape[1]))


def base_wave(turns):
    quarter = (turns - 0.5) * (0.5 * PI)
    square = quarter * quarter
    sine = quarter * (
        1.0 + square * (-1 / 6 + square * (1 / 120 + square * (-1 / 5040 + square * (1 / 362880))))
    )
    cosine = 1.0 + square * (
        -1 / 2 + square * (1 / 24 + square * (-1 / 720 + square * (1 / 40320 - square * (1 / 3628800))))
    )
    sine, cosine = 2.0 * sine * cosine, 1.0 - 2.0 * sine * sine
    sine, cosine = 2.0 * sine * cosine, 1.0 - 2.0 * sine * sine
    return -cosine, -sine


def times(left, right):
    return left[0] * right[0] - left[1] * right[1], left[1] * right[0] + left[0] * right[1]


def fold_kernel(recv_ref, lat_ref, table_ref, sum_ref):
    groups = lat_ref.shape[1]
    senders = recv_ref.shape[0] // groups
    rows = lat_ref.shape[2]
    tiles = rows // LANES

    sum_ref[...] = jnp.zeros_like(sum_ref)
    frequency = lax.broadcasted_iota(jnp.int32, (HALF, rows), 0)

    def fold(group, carry):
        both = recv_ref[group * senders].astype(F32)
        for sender in range(1, senders):
            both = both + recv_ref[group * senders + sender].astype(F32)
        c_real, c_imag = (jnp.concatenate([both[k + t : k + t + 1] for t in range(tiles)], axis=1) for k in (0, tiles))
        lat_a = lat_ref[0, pl.ds(group, 1), :]
        lat_b = lat_ref[1, pl.ds(group, 1), :]
        sign_a = jnp.where(lat_a < 0, -1.0, 1.0)
        sign_b = jnp.where(lat_b < 0, -1.0, 1.0)
        at_a = frequency == jnp.abs(lat_a)
        at_b = frequency == jnp.abs(lat_b)
        zero = jnp.zeros((), F32)
        left = jnp.concatenate(
            [
                jnp.where(at_a, value, zero).astype(BF16)
                for value in (c_real, c_real * sign_a, c_imag, c_imag * sign_a)
            ],
            axis=0,
        )
        right = jnp.concatenate(
            [jnp.where(at_b, value, zero).astype(BF16) for value in (jnp.ones_like(sign_b), sign_b)], axis=0
        )
        sum_ref[...] += lax.dot_general(left, right, (((1,), (1,)), ((), ())), preferred_element_type=F32)
        return carry

    lax.fori_loop(0, groups, fold, 0, unroll=4)
    real_even = sum_ref[0:HALF, :]
    real_odd = sum_ref[HALF : 2 * HALF, :]
    imag_even = sum_ref[2 * HALF : 3 * HALF, :]
    imag_odd = sum_ref[3 * HALF : 4 * HALF, :]
    even = lax.broadcasted_iota(jnp.int32, real_even.shape, 1) < HALF
    table = jnp.concatenate(
        [
            jnp.where(even, real_even, -imag_even),
            jnp.where(even, -imag_odd, -real_odd),
            jnp.where(even, imag_even, real_even),
            jnp.where(even, real_odd, -imag_odd),
        ],
        axis=0,
    )
    high = table.astype(BF16).astype(F32)
    low = table - high
    pad = jnp.zeros((4 * HALF, table_ref.shape[1] - 6 * HALF), F32)
    table_ref[...] = jnp.concatenate([high, high, low, pad], axis=1).astype(BF16)


def orbital_kernel(table_ref, pos_ref, out_ref, wave_ref, eight_ref, group_ref, chunk_ref, *, unroll, each):
    groups = out_ref.shape[0]
    chunks = out_ref.shape[1] // 2
    own = RUN // LANES
    runs = chunks // own
    upper = lax.axis_index("band") < lax.axis_size("band") // 2
    walk = lax.axis_index("walk")
    active = walk < each
    out_ref[...] = jnp.zeros_like(out_ref)

    def waves(group, length):
        away = group ^ walk
        for line in range(0, 2 * chunks, 8):
            first = base_wave(pos_ref[away, line : line + 8, :])
            power = (jnp.ones((8, LANES), F32), jnp.zeros((8, LANES), F32))
            for k in range(8):
                for half in range(2):
                    wave_ref[half, group, pl.ds(line * 8 + k, 8, stride=8), :] = power[half]
                power = first if k == 0 else times(power, first)
            for half in range(2):
                eight_ref[half, group, line : line + 8, :] = power[half]
        numbers = pos_ref[away, 2 * chunks : 2 * chunks + runs, :].astype(jnp.int32)
        for run in range(runs):
            number = numbers[run, 0]
            low = jnp.where(upper, 0, number // LANES)
            high = jnp.where(upper, (number + LANES - 1) // LANES, own)
            high = jnp.where(active, high, low)

            def note(chunk, at):
                group_ref[at] = group
                chunk_ref[at] = run * own + chunk
                return at + 1

            length = lax.fori_loop(low, high, note, length)
        return length

    length = lax.fori_loop(0, groups, waves, 0)

    def basis(entry, axis):
        group, chunk = entry
        line = axis * chunks + chunk
        start = pl.multiple_of(line * 8, 8)
        now = tuple(wave_ref[half, group, pl.ds(start, 8), :] for half in range(2))
        step = tuple(jnp.broadcast_to(eight_ref[half, group, pl.ds(line, 1), :], (8, LANES)) for half in range(2))
        twice = 2.0 * step[0]
        last, now = now, times(now, step)
        cosines, sines = [last[0], now[0]], [last[1], now[1]]
        for _ in range(2, HALF // 8):
            last, now = now, tuple(twice * now[half] - last[half] for half in range(2))
            cosines.append(now[0])
            sines.append(now[1])
        return jnp.concatenate(cosines + sines, axis=0)

    zeros = jnp.zeros((table_ref.shape[1] - 6 * HALF, 2 * LANES), BF16)

    def evaluate(index, carry):
        for inner in range(unroll):
            places = [jnp.minimum((index * unroll + inner) * 2 + side, length - 1) for side in range(2)]
            entries = [(group_ref[place], chunk_ref[place]) for place in places]
            wave_y = jnp.concatenate([basis(entry, 1) for entry in entries], axis=1)
            high_y = wave_y.astype(BF16)
            low_y = (wave_y - high_y.astype(F32)).astype(BF16)
            weights = jnp.concatenate([high_y, low_y, high_y, zeros], axis=0)
            inside = jnp.dot(table_ref[...], weights, preferred_element_type=F32)
            wave_x = jnp.concatenate([basis(entry, 0) for entry in entries], axis=1)
            for half in range(2):
                value = jnp.sum(inside[half * 2 * HALF : (half + 1) * 2 * HALF, :] * wave_x, axis=0, keepdims=True)
                for side, (group, chunk) in enumerate(entries):
                    out_ref[group, pl.ds(half * chunks + chunk, 1), :] = value[:, side * LANES : (side + 1) * LANES]
        return carry

    lax.fori_loop(0, (length + 2 * unroll - 1) // (2 * unroll), evaluate, 0)


def gradient_kernel(target_ref, feature_ref, net_hbm, out_ref, net_ref, sem, *, scale):
    copy = pltpu.make_async_copy(net_hbm, net_ref, sem)
    copy.start()
    chunks = feature_ref.shape[0] // LANES
    slots = out_ref.shape[0] // 2
    upper = lax.axis_index("band") < lax.axis_size("band") // 2
    targets = [
        jnp.concatenate(
            [target_ref[pl.ds(half * chunks + chunk, slots, stride=2 * chunks), :] for chunk in range(chunks)], axis=1
        )
        for half in range(2)
    ]
    copy.wait()
    mine = net_ref[2 * slots : 2 * slots + 1, :] == jnp.where(upper, 1.0, 0.0)
    parts = []
    for half in range(2):
        scaled = (net_ref[half * slots : (half + 1) * slots, :] - targets[half]) * scale
        parts.append(jnp.where(mine, scaled, 0.0))
    spread = jnp.concatenate(parts, axis=0)
    total = jnp.zeros(out_ref.shape, F32)
    for piece in split3(spread):
        total = total + jnp.dot(piece, feature_ref[...], preferred_element_type=F32)
    out_ref[...] = total


def call(kernel, out, scratch=(), mebibytes=16, **more):
    return pl.pallas_call(
        kernel,
        out_shape=out,
        **more,
        scratch_shapes=list(scratch),
        interpret=INTERPRET,
        compiler_params=pltpu.CompilerParams(vmem_limit_bytes=mebibytes * 1024 * 1024),
    )


def local(positions, coefficients, lattice, spin_labels, occupied, features, orbital_head):
    walk_count = lax.axis_size("walk")
    band_count = lax.axis_size("band")
    band_index = lax.axis_index("band")
    devices = walk_count * band_count
    rows = coefficients.shape[1]
    count = positions.shape[1]
    orbitals = occupied.shape[0] * occupied.shape[1]
    each = orbitals // band_count

    chunks = count // LANES
    anywhere = pl.BlockSpec(memory_space=pltpu.HBM)
    picked = call(
        pick_kernel,
        jax.ShapeDtypeStruct((devices * BLOCK, LANES), BF16),
        [
            pltpu.VMEM(coefficients.shape, BF16),
            pltpu.SMEM(occupied.shape, jnp.int32),
            pltpu.VMEM((devices * BLOCK, LANES), F32),
            pltpu.SemaphoreType.DMA((3,)),
        ],
        in_specs=[anywhere, anywhere],
    )(pltpu.with_memory_space_constraint(coefficients, pltpu.HBM), pltpu.with_memory_space_constraint(occupied, pltpu.HBM))
    picked, positions = lax.optimization_barrier((picked, positions))
    received = lax.all_to_all(picked.reshape(devices, BLOCK, LANES), ("walk", "band"), 0, 0, tiled=True)
    ordered, slot, up = call(
        order_kernel,
        (
            jax.ShapeDtypeStruct((2 * chunks + 8, LANES), F32),
            jax.ShapeDtypeStruct((count // RUN, RUN), F32),
            jax.ShapeDtypeStruct((1, count), F32),
        ),
    )(positions, spin_labels.reshape(chunks, LANES))
    everyone = ordered[None]
    for flips in ((1,), tuple(range(2, walk_count, 2))):
        moved = [lax.ppermute(everyone, "walk", [(k, k ^ flip) for k in range(walk_count)]) for flip in flips]
        everyone = jnp.concatenate([everyone, *moved], axis=0)
    table = call(
        fold_kernel, jax.ShapeDtypeStruct((4 * HALF, 512), BF16), [pltpu.VMEM((4 * HALF, 2 * HALF), F32)]
    )(received, lattice.reshape(2, walk_count, rows))
    values = call(
        functools.partial(orbital_kernel, unroll=8, each=each),
        jax.ShapeDtypeStruct((walk_count, 2 * chunks, LANES), F32),
        [
            pltpu.VMEM((2, walk_count, 16 * chunks, LANES), F32),
            pltpu.VMEM((2, walk_count, 2 * chunks, LANES), F32),
            pltpu.SMEM((walk_count * chunks,), jnp.int32),
            pltpu.SMEM((walk_count * chunks,), jnp.int32),
        ],
        mebibytes=24,
    )(table, everyone)
    target = lax.all_to_all(values, "walk", 0, 0, tiled=True).reshape(-1, LANES)

    spins = occupied.shape[0]
    per_spin = band_count // spins
    spin = band_index // per_spin
    columns = orbital_head.reshape(orbital_head.shape[0], spins, 2, per_spin, each)
    columns = lax.dynamic_index_in_dim(columns, spin, 1, keepdims=False)
    columns = lax.dynamic_index_in_dim(columns, band_index % per_spin, 2, keepdims=False)
    columns = jnp.transpose(columns, (1, 2, 0))
    columns = jnp.pad(columns, ((0, 0), (0, walk_count - each), (0, 0))).reshape(2 * walk_count, -1)
    sorted_features, net = call(
        sort_kernel,
        (jax.ShapeDtypeStruct(features.shape, BF16), jax.ShapeDtypeStruct((2 * walk_count + 8, count), F32)),
    )(slot, features, columns, up)
    net = pltpu.with_memory_space_constraint(net, pltpu.HBM)
    walkers = walk_count * count // orbitals
    hidden = features.shape[1]
    in_vmem = pl.BlockSpec(memory_space=pltpu.VMEM)
    own = call(
        functools.partial(gradient_kernel, scale=1.0 / walkers),
        jax.ShapeDtypeStruct((2 * walk_count, hidden), F32),
        [pltpu.VMEM(net.shape, F32), pltpu.SemaphoreType.DMA],
        in_specs=[in_vmem, in_vmem, anywhere],
    )(target, sorted_features, net)
    own = own.reshape(2, walk_count, hidden)[:, :each].reshape(-1, LANES)
    own = own + lax.ppermute(own, "walk", [(k, k ^ 1) for k in range(walk_count)])
    chips = walk_count // 2
    shares = lax.all_to_all(
        jnp.broadcast_to(own, (chips, *own.shape)),
        "walk",
        0,
        0,
        axis_index_groups=[[2 * chip + core for chip in range(chips)] for core in range(2)],
        tiled=True,
    )
    summed = jnp.sum(shares, axis=0)
    whole = lax.all_to_all(jnp.broadcast_to(summed, (band_count, *own.shape)), "band", 0, 0, tiled=True)
    whole = whole.reshape(spins, per_spin, 2, each, hidden)
    return jnp.transpose(whole, (4, 0, 2, 1, 3)).reshape(hidden, 2 * orbitals)


def solution(mesh):
    return jax.shard_map(
        local,
        mesh=mesh,
        in_specs=(
            P(None, "walk"),
            P(None, "walk", "band"),
            P(),
            P("walk"),
            P(),
            P("walk", None),
            P(),
        ),
        out_specs=P(),
        check_vma=False,
    )
```

profile of v0, /device:TPU:0, one launch (start us, length us, event | category | flops | bytes accessed | tf_op | source)
XLA Modules:
  0.0 108.8 jit_solution(1866560925984029969)
XLA Ops:
  0.0 2.6 %shard_map.73 = bf16[3072,128]{1,0:T(8,128)(2,1)} custom-call(bf16[2,1152,128]{2,1,0:T(8,128)(2,1)} %coef_hbm.1, s32[2,48]{1,0:T(2,128)} %occ_hbm.1), custom_call_target="tpu_custom_call" | custom-call | tf_op jit(solution)/shard_map/pallas_call | solution.py:314
  2.6 11.2 %all-to-all-start = ((bf16[128,24,128]{2,1,0:T(8,128)(2,1)}), bf16[128,24,128]{2,1,0:T(8,128)(2,1)S(1)}, u32[]{:S(2)}, u32[]{:S(2)}) async-start(bf16[128,24,128]{2,1,0:T(8,128)(2,1)} %bitcast), calls=%async_computation | async-start | bytes 1572864 | tf_op jit(solution)/shard_map/all_to_all | solution.py:326
  13.8 2.1 %shard_map.75 = (f32[56,128]{1,0:T(8,128)S(1)}, f32[3,1024]{1,0:T(4,128)S(1)}, f32[1,3072]{1,0:T(1,128)S(1)}) custom-call(f32[2,3072]{1,0:T(2,128)S(1)} %copy-done.4, s32[24,128]{1,0:T(8,128)S(1)} %bitcast.27), custom_call_target="tpu_custom_call" | custom-call | tf_op jit(solution)/shard_map/pallas_call | solution.py:327
  15.8 0.0 collective-permute-start
  15.9 1.2 %collective-permute-done = f32[1,56,128]{2,1,0:T(8,128)S(1)} collective-permute-done((f32[1,56,128]{2,1,0:T(8,128)S(1)}, f32[1,56,128]{2,1,0:T(8,128)S(1)}, u32[]{:S(2)}, u32[]{:S(2)}) %collective-permute-start) | collective-permute-done | bytes 28704 | tf_op jit(solution)/shard_map/ppermute | solution.py:337
  17.1 5.4 %collective-permute-start.7 = (f32[2,56,128]{2,1,0:T(8,128)S(1)}, f32[2,56,128]{2,1,0:T(8,128)S(1)}, u32[]{:S(2)}, u32[]{:S(2)}) collective-permute-start(f32[2,56,128]{2,1,0:T(8,128)S(1)} %pad_maximum_fusion), channel_id=1, source_target_pairs={{0,112},{8,120},{16,96},{24,104},{32,80},{40,88},{48,64},{56,72},{... | collective-permute-start | bytes 172040 | tf_op jit(solution)/shard_map/ppermute | solution.py:337
  22.4 0.2 collective-permute-start.6
  22.6 2.9 %collective-permute-start.5 = (f32[2,56,128]{2,1,0:T(8,128)S(1)}, f32[2,56,128]{2,1,0:T(8,128)S(1)}, u32[]{:S(2)}, u32[]{:S(2)}) collective-permute-start(f32[2,56,128]{2,1,0:T(8,128)S(1)} %pad_maximum_fusion), channel_id=1, source_target_pairs={{0,80},{8,88},{16,64},{24,72},{32,112},{40,120},{48,96},{56,104},{... | collective-permute-start | bytes 172040 | tf_op jit(solution)/shard_map/ppermute | solution.py:337
  25.5 1.1 collective-permute-start.4
  26.5 1.1 collective-permute-start.1
  27.6 3.9 %collective-permute-done.1 = f32[2,56,128]{2,1,0:T(8,128)S(1)} collective-permute-done((f32[2,56,128]{2,1,0:T(8,128)S(1)}, f32[2,56,128]{2,1,0:T(8,128)S(1)}, u32[]{:S(2)}, u32[]{:S(2)}) %collective-permute-start.1) | collective-permute-done | bytes 57376 | tf_op jit(solution)/shard_map/ppermute | solution.py:337
  31.5 3.0 %collective-permute-start.2 = (f32[2,56,128]{2,1,0:T(8,128)S(1)}, f32[2,56,128]{2,1,0:T(8,128)S(1)}, u32[]{:S(2)}, u32[]{:S(2)}) collective-permute-start(f32[2,56,128]{2,1,0:T(8,128)S(1)} %pad_maximum_fusion), channel_id=1, source_target_pairs={{0,32},{8,40},{16,48},{24,56},{32,0},{40,8},{48,16},{56,24},{64,96... | collective-permute-start | bytes 172040 | tf_op jit(solution)/shard_map/ppermute | solution.py:337
  34.5 2.7 %collective-permute-done.2 = f32[2,56,128]{2,1,0:T(8,128)S(1)} collective-permute-done((f32[2,56,128]{2,1,0:T(8,128)S(1)}, f32[2,56,128]{2,1,0:T(8,128)S(1)}, u32[]{:S(2)}, u32[]{:S(2)}) %collective-permute-start.2) | collective-permute-done | bytes 57376 | tf_op jit(solution)/shard_map/ppermute | solution.py:337
  37.2 2.3 %collective-permute-start.3 = (f32[2,56,128]{2,1,0:T(8,128)S(1)}, f32[2,56,128]{2,1,0:T(8,128)S(1)}, u32[]{:S(2)}, u32[]{:S(2)}) collective-permute-start(f32[2,56,128]{2,1,0:T(8,128)S(1)} %pad_maximum_fusion), channel_id=1, source_target_pairs={{0,48},{8,56},{16,32},{24,40},{32,16},{40,24},{48,0},{56,8},{64,11... | collective-permute-start | bytes 172040 | tf_op jit(solution)/shard_map/ppermute | solution.py:337
  39.4 3.1 %collective-permute-done.3 = f32[2,56,128]{2,1,0:T(8,128)S(1)} collective-permute-done((f32[2,56,128]{2,1,0:T(8,128)S(1)}, f32[2,56,128]{2,1,0:T(8,128)S(1)}, u32[]{:S(2)}, u32[]{:S(2)}) %collective-permute-start.3) | collective-permute-done | bytes 57376 | tf_op jit(solution)/shard_map/ppermute | solution.py:337
  42.7 0.0 copy-start.7
  42.7 0.0 copy-start
  42.7 4.7 %shard_map.74.table_ref = bf16[320,512]{1,0:T(8,128)(2,1)S(1)} custom-call(bf16[128,24,128]{2,1,0:T(8,128)(2,1)S(1)} %all-to-all-done.recv_ref, s32[2,16,1152]{2,1,0:T(8,128)S(1)} %bitcast.22), custom_call_target="tpu_custom_call" | custom-call | tf_op jit(solution)/shard_map/pallas_call | solution.py:339
  47.5 18.4 %shard_map.76 = f32[16,48,128]{2,1,0:T(8,128)} custom-call(bf16[320,512]{1,0:T(8,128)(2,1)S(1)} %shard_map.74.table_ref, f32[16,56,128]{2,1,0:T(8,128)S(1)} %constant_dynamic-update-slice_fusion.pos_ref), custom_call_target="tpu_custom_call" | custom-call | tf_op jit(solution)/shard_map/pallas_call | solution.py:342
  65.8 3.6 %all-to-all-start.1 = ((f32[16,48,128]{2,1,0:T(8,128)}), f32[16,48,128]{2,1,0:T(8,128)S(1)}, u32[]{:S(2)}, u32[]{:S(2)}) async-start(f32[16,48,128]{2,1,0:T(8,128)} %shard_map.76), calls=%async_computation.1 | async-start | bytes 786432 | tf_op jit(solution)/shard_map/all_to_all | solution.py:353
  69.6 3.4 %shard_map.77 = (bf16[3072,256]{1,0:T(8,128)(2,1)S(1)}, f32[40,3072]{1,0:T(8,128)S(1)}) custom-call(f32[3,1024]{1,0:T(4,128)S(1)} %get-tuple-element.15.slot_ref, bf16[3072,256]{1,0:T(8,128)(2,1)S(1)} %copy-done, bf16[32,256]{1,0:T(8,128)(2,1)S(1)} %bitcast.26, f32[1,3072]{1,0:T(1,128)S(1)} %get-tuple-element.16.up_ref), custom_call_target="tpu_custom_call" | custom-call | tf_op jit(solution)/shard_map/pallas_call | solution.py:363
  73.0 1.2 %copy-done.1 = bf16[3072,256]{1,0:T(8,128)(2,1)} copy-done((bf16[3072,256]{1,0:T(8,128)(2,1)}, bf16[3072,256]{1,0:T(8,128)(2,1)S(1)}, u32[]{:S(2)}) %copy-start.1) | copy-done | bytes 1572888
  74.2 0.8 copy-done.3
  75.0 5.4 %all-to-all-done.1 = f32[16,48,128]{2,1,0:T(8,128)S(1)} async-done(((f32[16,48,128]{2,1,0:T(8,128)}), f32[16,48,128]{2,1,0:T(8,128)S(1)}, u32[]{:S(2)}, u32[]{:S(2)}) %all-to-all-start.1) | async-done | bytes 393248 | tf_op jit(solution)/shard_map/all_to_all | solution.py:353
  80.4 1.4 %copy-done.2 = bf16[3072,256]{1,0:T(8,128)(2,1)S(1)} copy-done((bf16[3072,256]{1,0:T(8,128)(2,1)S(1)}, bf16[3072,256]{1,0:T(8,128)(2,1)}, u32[]{:S(2)}) %copy-start.2) | copy-done | bytes 1572888
  81.8 1.9 %shard_map.78 = f32[32,256]{1,0:T(8,128)S(1)} custom-call(f32[768,128]{1,0:T(8,128)S(1)} %bitcast.21, bf16[3072,256]{1,0:T(8,128)(2,1)S(1)} %copy-done.2, f32[40,3072]{1,0:T(8,128)} %copy-done.3), custom_call_target="tpu_custom_call" | custom-call | tf_op jit(solution)/shard_map/pallas_call | solution.py:371
  83.8 0.1 collective-permute-start.8
  83.8 1.2 %collective-permute-done.8 = f32[48,128]{1,0:T(8,128)S(1)} collective-permute-done((f32[48,128]{1,0:T(8,128)S(1)}, f32[48,128]{1,0:T(8,128)S(1)}, u32[]{:S(2)}, u32[]{:S(2)}) %collective-permute-start.8) | collective-permute-done | bytes 24608 | tf_op jit(solution)/shard_map/ppermute | solution.py:378
  85.1 11.1 %all_to_all.20 = f32[8,48,128]{2,1,0:T(8,128)S(1)} all-to-all(f32[8,48,128]{2,1,0:T(8,128)S(1)} %broadcast_in_dim.10), channel_id=1, replica_groups={{0,16,32,48,64,80,96,112},{8,24,40,56,72,88,104,120},{1,17,33,49,65,81,..., dimensions={0} | all-to-all | bytes 393216 | tf_op jit(solution)/shard_map/all_to_all | solution.py:380
  96.2 11.8 %all_to_all.21 = f32[8,48,128]{2,1,0:T(8,128)S(1)} all-to-all(f32[8,48,128]{2,1,0:T(8,128)S(1)} %broadcast_in_dim.11), channel_id=1, replica_groups=mesh['walk'=16,'band'=8] {'band'}, dimensions={0} | all-to-all | bytes 393216 | tf_op jit(solution)/shard_map/all_to_all | solution.py:389
  108.0 0.1 reshape.40
  108.1 0.7 reshape.41
  (36 shorter events, 0.2 us)
Async XLA Ops:
  0.0 13.7 %copy-start.4 = (f32[2,3072]{1,0:T(2,128)S(1)}, f32[2,3072]{1,0:T(2,128)}, u32[]{:S(2)}) copy-start(f32[2,3072]{1,0:T(2,128)} %pos_ref) | copy-start | bytes 73732
  0.0 13.8 %copy-start.5 = (s32[3072]{0:T(1024)S(1)}, s32[3072]{0:T(1024)}, u32[]{:S(2)}) copy-start(s32[3072]{0:T(1024)} %param.10) | copy-start | bytes 36868
  0.0 15.9 %copy-start.6 = (s32[2,18432]{1,0:T(2,128)S(1)}, s32[2,18432]{1,0:T(2,128)}, u32[]{:S(2)}) copy-start(s32[2,18432]{1,0:T(2,128)} %param.9) | copy-start | bytes 442372
  2.6 40.1 %all-to-all-start = ((bf16[128,24,128]{2,1,0:T(8,128)(2,1)}), bf16[128,24,128]{2,1,0:T(8,128)(2,1)S(1)}, u32[]{:S(2)}, u32[]{:S(2)}) async-start(bf16[128,24,128]{2,1,0:T(8,128)(2,1)} %bitcast), calls=%async_computation | async-start | bytes 1572864 | tf_op jit(solution)/shard_map/all_to_all | solution.py:326
  15.8 1.2 %collective-permute-start = (f32[1,56,128]{2,1,0:T(8,128)S(1)}, f32[1,56,128]{2,1,0:T(8,128)S(1)}, u32[]{:S(2)}, u32[]{:S(2)}) collective-permute-start(f32[1,56,128]{2,1,0:T(8,128)S(1)} %bitcast.24), channel_id=1, source_target_pairs={{0,8},{8,0},{16,24},{24,16},{32,40},{40,32},{48,56},{56,48},{64,72... | collective-permute-start | bytes 86024 | tf_op jit(solution)/shard_map/ppermute | solution.py:337
  17.1 25.6 %collective-permute-start.7 = (f32[2,56,128]{2,1,0:T(8,128)S(1)}, f32[2,56,128]{2,1,0:T(8,128)S(1)}, u32[]{:S(2)}, u32[]{:S(2)}) collective-permute-start(f32[2,56,128]{2,1,0:T(8,128)S(1)} %pad_maximum_fusion), channel_id=1, source_target_pairs={{0,112},{8,120},{16,96},{24,104},{32,80},{40,88},{48,64},{56,72},{... | collective-permute-start | bytes 172040 | tf_op jit(solution)/shard_map/ppermute | solution.py:337
  22.4 20.2 %collective-permute-start.6 = (f32[2,56,128]{2,1,0:T(8,128)S(1)}, f32[2,56,128]{2,1,0:T(8,128)S(1)}, u32[]{:S(2)}, u32[]{:S(2)}) collective-permute-start(f32[2,56,128]{2,1,0:T(8,128)S(1)} %pad_maximum_fusion), channel_id=1, source_target_pairs={{0,96},{8,104},{16,112},{24,120},{32,64},{40,72},{48,80},{56,88},{... | collective-permute-start | bytes 172040 | tf_op jit(solution)/shard_map/ppermute | solution.py:337
  22.6 20.0 %collective-permute-start.5 = (f32[2,56,128]{2,1,0:T(8,128)S(1)}, f32[2,56,128]{2,1,0:T(8,128)S(1)}, u32[]{:S(2)}, u32[]{:S(2)}) collective-permute-start(f32[2,56,128]{2,1,0:T(8,128)S(1)} %pad_maximum_fusion), channel_id=1, source_target_pairs={{0,80},{8,88},{16,64},{24,72},{32,112},{40,120},{48,96},{56,104},{... | collective-permute-start | bytes 172040 | tf_op jit(solution)/shard_map/ppermute | solution.py:337
  25.5 17.1 %collective-permute-start.4 = (f32[2,56,128]{2,1,0:T(8,128)S(1)}, f32[2,56,128]{2,1,0:T(8,128)S(1)}, u32[]{:S(2)}, u32[]{:S(2)}) collective-permute-start(f32[2,56,128]{2,1,0:T(8,128)S(1)} %pad_maximum_fusion), channel_id=1, source_target_pairs={{0,64},{8,72},{16,80},{24,88},{32,96},{40,104},{48,112},{56,120},{... | collective-permute-start | bytes 172040 | tf_op jit(solution)/shard_map/ppermute | solution.py:337
  26.5 5.0 %collective-permute-start.1 = (f32[2,56,128]{2,1,0:T(8,128)S(1)}, f32[2,56,128]{2,1,0:T(8,128)S(1)}, u32[]{:S(2)}, u32[]{:S(2)}) collective-permute-start(f32[2,56,128]{2,1,0:T(8,128)S(1)} %pad_maximum_fusion), channel_id=1, source_target_pairs={{0,16},{8,24},{16,0},{24,8},{32,48},{40,56},{48,32},{56,40},{64,80... | collective-permute-start | bytes 172040 | tf_op jit(solution)/shard_map/ppermute | solution.py:337
  31.5 5.7 %collective-permute-start.2 = (f32[2,56,128]{2,1,0:T(8,128)S(1)}, f32[2,56,128]{2,1,0:T(8,128)S(1)}, u32[]{:S(2)}, u32[]{:S(2)}) collective-permute-start(f32[2,56,128]{2,1,0:T(8,128)S(1)} %pad_maximum_fusion), channel_id=1, source_target_pairs={{0,32},{8,40},{16,48},{24,56},{32,0},{40,8},{48,16},{56,24},{64,96... | collective-permute-start | bytes 172040 | tf_op jit(solution)/shard_map/ppermute | solution.py:337
  37.2 5.4 %collective-permute-start.3 = (f32[2,56,128]{2,1,0:T(8,128)S(1)}, f32[2,56,128]{2,1,0:T(8,128)S(1)}, u32[]{:S(2)}, u32[]{:S(2)}) collective-permute-start(f32[2,56,128]{2,1,0:T(8,128)S(1)} %pad_maximum_fusion), channel_id=1, source_target_pairs={{0,48},{8,56},{16,32},{24,40},{32,16},{40,24},{48,0},{56,8},{64,11... | collective-permute-start | bytes 172040 | tf_op jit(solution)/shard_map/ppermute | solution.py:337
  42.7 26.8 %copy-start.7 = (bf16[256,192]{0,1:T(8,128)(2,1)S(1)}, bf16[256,192]{0,1:T(8,128)(2,1)}, u32[]{:S(2)}) copy-start(bf16[256,192]{0,1:T(8,128)(2,1)} %param.13) | copy-start | bytes 294916
  42.7 26.9 %copy-start = (bf16[3072,256]{1,0:T(8,128)(2,1)S(1)}, bf16[3072,256]{1,0:T(8,128)(2,1)}, u32[]{:S(2)}) copy-start(bf16[3072,256]{1,0:T(8,128)(2,1)} %feature_ref.1) | copy-start | bytes 4718596
  65.8 14.6 %all-to-all-start.1 = ((f32[16,48,128]{2,1,0:T(8,128)}), f32[16,48,128]{2,1,0:T(8,128)S(1)}, u32[]{:S(2)}, u32[]{:S(2)}) async-start(f32[16,48,128]{2,1,0:T(8,128)} %shard_map.76), calls=%async_computation.1 | async-start | bytes 786432 | tf_op jit(solution)/shard_map/all_to_all | solution.py:353
  73.0 1.2 %copy-start.1 = (bf16[3072,256]{1,0:T(8,128)(2,1)}, bf16[3072,256]{1,0:T(8,128)(2,1)S(1)}, u32[]{:S(2)}) copy-start(bf16[3072,256]{1,0:T(8,128)(2,1)S(1)} %get-tuple-element.17.feature_ref) | copy-start | bytes 4718596
  74.2 0.8 copy-start.3
  80.4 1.4 %copy-start.2 = (bf16[3072,256]{1,0:T(8,128)(2,1)S(1)}, bf16[3072,256]{1,0:T(8,128)(2,1)}, u32[]{:S(2)}) copy-start(bf16[3072,256]{1,0:T(8,128)(2,1)} %copy-done.1) | copy-start | bytes 4718596
  83.8 1.3 %collective-permute-start.8 = (f32[48,128]{1,0:T(8,128)S(1)}, f32[48,128]{1,0:T(8,128)S(1)}, u32[]{:S(2)}, u32[]{:S(2)}) collective-permute-start(f32[48,128]{1,0:T(8,128)S(1)} %reshape.39), channel_id=1, source_target_pairs={{0,8},{8,0},{16,24},{24,16},{32,40},{40,32},{48,56},{56,48},{64,72... | collective-permute-start | bytes 73736 | tf_op jit(solution)/shard_map/ppermute | solution.py:378
where the time goes:
time: 109 us
  Pallas kernels  33.1 us (30%)
  starting transfers between devices  30.7 us (28%)
  blocking collectives  22.9 us (21%)
  waiting for transfers between devices  17.5 us (16%)
  local copies, waits for them, and re-layouts  4.35 us (4%)
    pallas_call x1, Pallas kernels, local(): call(functools.partial(orbital_kernel, unroll=8, each=each), jax.ShapeDty...  18.4 us
    ppermute x8, starting transfers between devices, local(): lax.ppermute(everyone, 'walk', [(k, k ^ flip) for k in range(walk_count)])  15.8 us
    all_to_all x1, blocking collectives, local(): lax.all_to_all(jnp.broadcast_to(summed, (band_count, *own.shape)), 'band'...  11.8 us
    all_to_all x1, starting transfers between devices, local(): lax.all_to_all(picked.reshape(devices, BLOCK, LANES), ('walk', 'band'), 0...  11.2 us
    all_to_all x1, blocking collectives, local(): lax.all_to_all(jnp.broadcast_to(own, (chips, *own.shape)), 'walk', 0, 0,...  11.1 us
    ppermute x8, waiting for transfers between devices, local(): lax.ppermute(everyone, 'walk', [(k, k ^ flip) for k in range(walk_count)])  10.9 us
    all_to_all x1, waiting for transfers between devices, local(): target = lax.all_to_all(values, 'walk', 0, 0, tiled=True).reshape(-1, LANES)  5.41 us
    pallas_call x1, Pallas kernels, local(): call(fold_kernel, jax.ShapeDtypeStruct((4 * HALF, 512), BF16), [pltpu.VME...  4.74 us
  transfers between devices with their start and end apart: 11, of which 6 were waited for; matrix products, arithmetic and copies ran while one was open for 0% of the time, Pallas kernels for 5%

commit v1 on v0

--- a/solution.py
+++ b/solution.py
@@ -86,11 +86,11 @@
     first = jnp.where(place < total, 1.0, 0.0)
     up_ref[...] = jnp.concatenate([first[chunk : chunk + 1, :] for chunk in range(chunks)], axis=1)
     parts = jnp.concatenate([part.astype(F32) for part in split3(pos_ref[...])], axis=0).astype(BF16)
-    here = lax.broadcasted_iota(jnp.int32, (RUN, RUN), 0).astype(F32)
+    here = lax.broadcasted_iota(jnp.int16, (RUN, RUN), 0)
     for run in range(runs):
         line = jnp.concatenate([slot[run * own + k : run * own + k + 1, :] for k in range(own)], axis=1)
         slot_ref[run : run + 1, :] = line
-        move = jnp.where(here == line, 1.0, 0.0).astype(BF16)
+        move = jnp.where(here == line.astype(jnp.int32).astype(jnp.int16), jnp.ones((), BF16), jnp.zeros((), BF16))
         moved = lax.dot_general(
             parts[:, run * RUN : (run + 1) * RUN], move, (((1,), (1,)), ((), ())), preferred_element_type=F32
         )
@@ -141,7 +141,7 @@
     tiles = rows // LANES
 
     sum_ref[...] = jnp.zeros_like(sum_ref)
-    frequency = lax.broadcasted_iota(jnp.int32, (HALF, rows), 0)
+    frequency = lax.broadcasted_iota(jnp.int16, (HALF, rows), 0)
 
     def fold(group, carry):
         both = recv_ref[group * senders].astype(F32)
@@ -152,23 +152,23 @@
         lat_b = lat_ref[1, pl.ds(group, 1), :]
         sign_a = jnp.where(lat_a < 0, -1.0, 1.0)
         sign_b = jnp.where(lat_b < 0, -1.0, 1.0)
-        at_a = frequency == jnp.abs(lat_a)
-        at_b = frequency == jnp.abs(lat_b)
-        zero = jnp.zeros((), F32)
+        at_a = frequency == jnp.abs(lat_a).astype(jnp.int16)
+        at_b = frequency == jnp.abs(lat_b).astype(jnp.int16)
+        zero = jnp.zeros((), BF16)
         left = jnp.concatenate(
             [
-                jnp.where(at_a, value, zero).astype(BF16)
+                jnp.where(at_a, value.astype(BF16), zero)
                 for value in (c_real, c_real * sign_a, c_imag, c_imag * sign_a)
             ],
             axis=0,
         )
         right = jnp.concatenate(
-            [jnp.where(at_b, value, zero).astype(BF16) for value in (jnp.ones_like(sign_b), sign_b)], axis=0
+            [jnp.where(at_b, value.astype(BF16), zero) for value in (jnp.ones_like(sign_b), sign_b)], axis=0
         )
         sum_ref[...] += lax.dot_general(left, right, (((1,), (1,)), ((), ())), preferred_element_type=F32)
         return carry
 
-    lax.fori_loop(0, groups, fold, 0, unroll=4)
+    lax.fori_loop(0, groups, fold, 0, unroll=8)
     real_even = sum_ref[0:HALF, :]
     real_odd = sum_ref[HALF : 2 * HALF, :]
     imag_even = sum_ref[2 * HALF : 3 * HALF, :]
@@ -282,10 +282,10 @@
         scaled = (net_ref[half * slots : (half + 1) * slots, :] - targets[half]) * scale
         parts.append(jnp.where(mine, scaled, 0.0))
     spread = jnp.concatenate(parts, axis=0)
-    total = jnp.zeros(out_ref.shape, F32)
-    for piece in split3(spread):
-        total = total + jnp.dot(piece, feature_ref[...], preferred_element_type=F32)
-    out_ref[...] = total
+    pieces = jnp.concatenate([piece.astype(F32) for piece in split3(spread)], axis=0).astype(BF16)
+    total = jnp.dot(pieces, feature_ref[...], preferred_element_type=F32)
+    height = out_ref.shape[0]
+    out_ref[...] = total[:height] + total[height : 2 * height] + total[2 * height :]
 
 
 def call(kernel, out, scratch=(), mebibytes=16, **more):
@@ -340,7 +340,7 @@
         fold_kernel, jax.ShapeDtypeStruct((4 * HALF, 512), BF16), [pltpu.VMEM((4 * HALF, 2 * HALF), F32)]
     )(received, lattice.reshape(2, walk_count, rows))
     values = call(
-        functools.partial(orbital_kernel, unroll=8, each=each),
+        functools.partial(orbital_kernel, unroll=12, each=each),
         jax.ShapeDtypeStruct((walk_count, 2 * chunks, LANES), F32),
         [
             pltpu.VMEM((2, walk_count, 16 * chunks, LANES), F32),

time: 109 us -> 107 us (0.982)
  Pallas kernels: 33.1 us -> 32 us
where the time goes in v1:
time: 107 us
  Pallas kernels  32 us (30%)
  starting transfers between devices  30.7 us (29%)
  blocking collectives  22 us (21%)
  waiting for transfers between devices  17.5 us (16%)
  local copies, waits for them, and re-layouts  4.35 us (4%)
    pallas_call x1, Pallas kernels, local(): call(functools.partial(orbital_kernel, unroll=12, each=each), jax.ShapeDt...  18.3 us
    ppermute x8, starting transfers between devices, local(): lax.ppermute(everyone, 'walk', [(k, k ^ flip) for k in range(walk_count)])  15.8 us
    all_to_all x1, starting transfers between devices, local(): lax.all_to_all(picked.reshape(devices, BLOCK, LANES), ('walk', 'band'), 0...  11.2 us
    all_to_all x1, blocking collectives, local(): lax.all_to_all(jnp.broadcast_to(own, (chips, *own.shape)), 'walk', 0, 0,...  11.1 us
    all_to_all x1, blocking collectives, local(): lax.all_to_all(jnp.broadcast_to(summed, (band_count, *own.shape)), 'band'...  11 us
    ppermute x8, waiting for transfers between devices, local(): lax.ppermute(everyone, 'walk', [(k, k ^ flip) for k in range(walk_count)])  10.9 us
    all_to_all x1, waiting for transfers between devices, local(): target = lax.all_to_all(values, 'walk', 0, 0, tiled=True).reshape(-1, LANES)  5.41 us
    pallas_call x1, Pallas kernels, local(): call(fold_kernel, jax.ShapeDtypeStruct((4 * HALF, 512), BF16), [pltpu.VME...  4.2 us
  transfers between devices with their start and end apart: 11, of which 6 were waited for; matrix products, arithmetic and copies ran while one was open for 0% of the time, Pallas kernels for 5%

profile of v1, /device:TPU:0, one launch (start us, length us, event | category | flops | bytes accessed | tf_op | source)
XLA Modules:
  0.0 106.8 jit_solution(17437815319450137919)
XLA Ops:
  0.0 2.6 %shard_map.73 = bf16[3072,128]{1,0:T(8,128)(2,1)} custom-call(bf16[2,1152,128]{2,1,0:T(8,128)(2,1)} %coef_hbm.1, s32[2,48]{1,0:T(2,128)} %occ_hbm.1), custom_call_target="tpu_custom_call" | custom-call | tf_op jit(solution)/shard_map/pallas_call | solution.py:314
  2.6 11.2 %all-to-all-start = ((bf16[128,24,128]{2,1,0:T(8,128)(2,1)}), bf16[128,24,128]{2,1,0:T(8,128)(2,1)S(1)}, u32[]{:S(2)}, u32[]{:S(2)}) async-start(bf16[128,24,128]{2,1,0:T(8,128)(2,1)} %bitcast), calls=%async_computation | async-start | bytes 1572864 | tf_op jit(solution)/shard_map/all_to_all | solution.py:326
  13.8 2.1 %shard_map.75 = (f32[56,128]{1,0:T(8,128)S(1)}, f32[3,1024]{1,0:T(4,128)S(1)}, f32[1,3072]{1,0:T(1,128)S(1)}) custom-call(f32[2,3072]{1,0:T(2,128)S(1)} %copy-done.4, s32[24,128]{1,0:T(8,128)S(1)} %bitcast.27), custom_call_target="tpu_custom_call" | custom-call | tf_op jit(solution)/shard_map/pallas_call | solution.py:327
  15.9 1.2 %collective-permute-done = f32[1,56,128]{2,1,0:T(8,128)S(1)} collective-permute-done((f32[1,56,128]{2,1,0:T(8,128)S(1)}, f32[1,56,128]{2,1,0:T(8,128)S(1)}, u32[]{:S(2)}, u32[]{:S(2)}) %collective-permute-start) | collective-permute-done | bytes 28704 | tf_op jit(solution)/shard_map/ppermute | solution.py:337
  17.1 5.4 %collective-permute-start.7 = (f32[2,56,128]{2,1,0:T(8,128)S(1)}, f32[2,56,128]{2,1,0:T(8,128)S(1)}, u32[]{:S(2)}, u32[]{:S(2)}) collective-permute-start(f32[2,56,128]{2,1,0:T(8,128)S(1)} %pad_maximum_fusion), channel_id=1, source_target_pairs={{0,112},{8,120},{16,96},{24,104},{32,80},{40,88},{48,64},{56,72},{... | collective-permute-start | bytes 172040 | tf_op jit(solution)/shard_map/ppermute | solution.py:337
  22.4 0.2 collective-permute-start.6
  22.6 2.9 %collective-permute-start.5 = (f32[2,56,128]{2,1,0:T(8,128)S(1)}, f32[2,56,128]{2,1,0:T(8,128)S(1)}, u32[]{:S(2)}, u32[]{:S(2)}) collective-permute-start(f32[2,56,128]{2,1,0:T(8,128)S(1)} %pad_maximum_fusion), channel_id=1, source_target_pairs={{0,80},{8,88},{16,64},{24,72},{32,112},{40,120},{48,96},{56,104},{... | collective-permute-start | bytes 172040 | tf_op jit(solution)/shard_map/ppermute | solution.py:337
  25.5 1.1 collective-permute-start.4
  26.5 1.1 %collective-permute-start.1 = (f32[2,56,128]{2,1,0:T(8,128)S(1)}, f32[2,56,128]{2,1,0:T(8,128)S(1)}, u32[]{:S(2)}, u32[]{:S(2)}) collective-permute-start(f32[2,56,128]{2,1,0:T(8,128)S(1)} %pad_maximum_fusion), channel_id=1, source_target_pairs={{0,16},{8,24},{16,0},{24,8},{32,48},{40,56},{48,32},{56,40},{64,80... | collective-permute-start | bytes 172040 | tf_op jit(solution)/shard_map/ppermute | solution.py:337
  27.6 3.9 %collective-permute-done.1 = f32[2,56,128]{2,1,0:T(8,128)S(1)} collective-permute-done((f32[2,56,128]{2,1,0:T(8,128)S(1)}, f32[2,56,128]{2,1,0:T(8,128)S(1)}, u32[]{:S(2)}, u32[]{:S(2)}) %collective-permute-start.1) | collective-permute-done | bytes 57376 | tf_op jit(solution)/shard_map/ppermute | solution.py:337
  31.5 3.0 %collective-permute-start.2 = (f32[2,56,128]{2,1,0:T(8,128)S(1)}, f32[2,56,128]{2,1,0:T(8,128)S(1)}, u32[]{:S(2)}, u32[]{:S(2)}) collective-permute-start(f32[2,56,128]{2,1,0:T(8,128)S(1)} %pad_maximum_fusion), channel_id=1, source_target_pairs={{0,32},{8,40},{16,48},{24,56},{32,0},{40,8},{48,16},{56,24},{64,96... | collective-permute-start | bytes 172040 | tf_op jit(solution)/shard_map/ppermute | solution.py:337
  34.5 2.7 %collective-permute-done.2 = f32[2,56,128]{2,1,0:T(8,128)S(1)} collective-permute-done((f32[2,56,128]{2,1,0:T(8,128)S(1)}, f32[2,56,128]{2,1,0:T(8,128)S(1)}, u32[]{:S(2)}, u32[]{:S(2)}) %collective-permute-start.2) | collective-permute-done | bytes 57376 | tf_op jit(solution)/shard_map/ppermute | solution.py:337
  37.2 2.3 %collective-permute-start.3 = (f32[2,56,128]{2,1,0:T(8,128)S(1)}, f32[2,56,128]{2,1,0:T(8,128)S(1)}, u32[]{:S(2)}, u32[]{:S(2)}) collective-permute-start(f32[2,56,128]{2,1,0:T(8,128)S(1)} %pad_maximum_fusion), channel_id=1, source_target_pairs={{0,48},{8,56},{16,32},{24,40},{32,16},{40,24},{48,0},{56,8},{64,11... | collective-permute-start | bytes 172040 | tf_op jit(solution)/shard_map/ppermute | solution.py:337
  39.4 3.1 %collective-permute-done.3 = f32[2,56,128]{2,1,0:T(8,128)S(1)} collective-permute-done((f32[2,56,128]{2,1,0:T(8,128)S(1)}, f32[2,56,128]{2,1,0:T(8,128)S(1)}, u32[]{:S(2)}, u32[]{:S(2)}) %collective-permute-start.3) | collective-permute-done | bytes 57376 | tf_op jit(solution)/shard_map/ppermute | solution.py:337
  42.6 0.0 collective-permute-done.4
  42.7 0.0 copy-start.7
  42.7 0.0 copy-start
  42.7 4.2 %shard_map.74.table_ref = bf16[320,512]{1,0:T(8,128)(2,1)S(1)} custom-call(bf16[128,24,128]{2,1,0:T(8,128)(2,1)S(1)} %all-to-all-done.recv_ref, s32[2,16,1152]{2,1,0:T(8,128)S(1)} %bitcast.22), custom_call_target="tpu_custom_call" | custom-call | tf_op jit(solution)/shard_map/pallas_call | solution.py:339
  46.9 18.3 %shard_map.76 = f32[16,48,128]{2,1,0:T(8,128)} custom-call(bf16[320,512]{1,0:T(8,128)(2,1)S(1)} %shard_map.74.table_ref, f32[16,56,128]{2,1,0:T(8,128)S(1)} %constant_dynamic-update-slice_fusion.pos_ref), custom_call_target="tpu_custom_call" | custom-call | tf_op jit(solution)/shard_map/pallas_call | solution.py:342
  65.2 3.7 %all-to-all-start.1 = ((f32[16,48,128]{2,1,0:T(8,128)}), f32[16,48,128]{2,1,0:T(8,128)S(1)}, u32[]{:S(2)}, u32[]{:S(2)}) async-start(f32[16,48,128]{2,1,0:T(8,128)} %shard_map.76), calls=%async_computation.1 | async-start | bytes 786432 | tf_op jit(solution)/shard_map/all_to_all | solution.py:353
  69.0 3.4 %shard_map.77 = (bf16[3072,256]{1,0:T(8,128)(2,1)S(1)}, f32[40,3072]{1,0:T(8,128)S(1)}) custom-call(f32[3,1024]{1,0:T(4,128)S(1)} %get-tuple-element.15.slot_ref, bf16[3072,256]{1,0:T(8,128)(2,1)S(1)} %copy-done, bf16[32,256]{1,0:T(8,128)(2,1)S(1)} %bitcast.26, f32[1,3072]{1,0:T(1,128)S(1)} %get-tuple-element.16.up_ref), custom_call_target="tpu_custom_call" | custom-call | tf_op jit(solution)/shard_map/pallas_call | solution.py:363
  72.4 1.2 %copy-done.1 = bf16[3072,256]{1,0:T(8,128)(2,1)} copy-done((bf16[3072,256]{1,0:T(8,128)(2,1)}, bf16[3072,256]{1,0:T(8,128)(2,1)S(1)}, u32[]{:S(2)}) %copy-start.1) | copy-done | bytes 1572888
  73.6 0.8 copy-done.3
  74.4 5.4 %all-to-all-done.1 = f32[16,48,128]{2,1,0:T(8,128)S(1)} async-done(((f32[16,48,128]{2,1,0:T(8,128)}), f32[16,48,128]{2,1,0:T(8,128)S(1)}, u32[]{:S(2)}, u32[]{:S(2)}) %all-to-all-start.1) | async-done | bytes 393248 | tf_op jit(solution)/shard_map/all_to_all | solution.py:353
  79.8 1.4 %copy-done.2 = bf16[3072,256]{1,0:T(8,128)(2,1)S(1)} copy-done((bf16[3072,256]{1,0:T(8,128)(2,1)S(1)}, bf16[3072,256]{1,0:T(8,128)(2,1)}, u32[]{:S(2)}) %copy-start.2) | copy-done | bytes 1572888
  81.2 1.4 %shard_map.78 = f32[32,256]{1,0:T(8,128)S(1)} custom-call(f32[768,128]{1,0:T(8,128)S(1)} %bitcast.21, bf16[3072,256]{1,0:T(8,128)(2,1)S(1)} %copy-done.2, f32[40,3072]{1,0:T(8,128)} %copy-done.3), custom_call_target="tpu_custom_call" | custom-call | tf_op jit(solution)/shard_map/pallas_call | solution.py:371
  82.7 0.1 collective-permute-start.8
  82.8 1.2 %collective-permute-done.8 = f32[48,128]{1,0:T(8,128)S(1)} collective-permute-done((f32[48,128]{1,0:T(8,128)S(1)}, f32[48,128]{1,0:T(8,128)S(1)}, u32[]{:S(2)}, u32[]{:S(2)}) %collective-permute-start.8) | collective-permute-done | bytes 24608 | tf_op jit(solution)/shard_map/ppermute | solution.py:378
  84.0 11.1 %all_to_all.20 = f32[8,48,128]{2,1,0:T(8,128)S(1)} all-to-all(f32[8,48,128]{2,1,0:T(8,128)S(1)} %broadcast_in_dim.10), channel_id=1, replica_groups={{0,16,32,48,64,80,96,112},{8,24,40,56,72,88,104,120},{1,17,33,49,65,81,..., dimensions={0} | all-to-all | bytes 393216 | tf_op jit(solution)/shard_map/all_to_all | solution.py:380
  95.1 11.0 %all_to_all.21 = f32[8,48,128]{2,1,0:T(8,128)S(1)} all-to-all(f32[8,48,128]{2,1,0:T(8,128)S(1)} %broadcast_in_dim.11), channel_id=1, replica_groups=mesh['walk'=16,'band'=8] {'band'}, dimensions={0} | all-to-all | bytes 393216 | tf_op jit(solution)/shard_map/all_to_all | solution.py:389
  106.1 0.1 reshape.40
  106.1 0.7 reshape.41
  (36 shorter events, 0.2 us)
Async XLA Ops:
  0.0 13.7 %copy-start.4 = (f32[2,3072]{1,0:T(2,128)S(1)}, f32[2,3072]{1,0:T(2,128)}, u32[]{:S(2)}) copy-start(f32[2,3072]{1,0:T(2,128)} %pos_ref) | copy-start | bytes 73732
  0.0 13.8 %copy-start.5 = (s32[3072]{0:T(1024)S(1)}, s32[3072]{0:T(1024)}, u32[]{:S(2)}) copy-start(s32[3072]{0:T(1024)} %param.10) | copy-start | bytes 36868
  0.0 15.9 %copy-start.6 = (s32[2,18432]{1,0:T(2,128)S(1)}, s32[2,18432]{1,0:T(2,128)}, u32[]{:S(2)}) copy-start(s32[2,18432]{1,0:T(2,128)} %param.9) | copy-start | bytes 442372
  2.6 40.1 %all-to-all-start = ((bf16[128,24,128]{2,1,0:T(8,128)(2,1)}), bf16[128,24,128]{2,1,0:T(8,128)(2,1)S(1)}, u32[]{:S(2)}, u32[]{:S(2)}) async-start(bf16[128,24,128]{2,1,0:T(8,128)(2,1)} %bitcast), calls=%async_computation | async-start | bytes 1572864 | tf_op jit(solution)/shard_map/all_to_all | solution.py:326
  15.8 1.2 %collective-permute-start = (f32[1,56,128]{2,1,0:T(8,128)S(1)}, f32[1,56,128]{2,1,0:T(8,128)S(1)}, u32[]{:S(2)}, u32[]{:S(2)}) collective-permute-start(f32[1,56,128]{2,1,0:T(8,128)S(1)} %bitcast.24), channel_id=1, source_target_pairs={{0,8},{8,0},{16,24},{24,16},{32,40},{40,32},{48,56},{56,48},{64,72... | collective-permute-start | bytes 86024 | tf_op jit(solution)/shard_map/ppermute | solution.py:337
  17.1 25.6 %collective-permute-start.7 = (f32[2,56,128]{2,1,0:T(8,128)S(1)}, f32[2,56,128]{2,1,0:T(8,128)S(1)}, u32[]{:S(2)}, u32[]{:S(2)}) collective-permute-start(f32[2,56,128]{2,1,0:T(8,128)S(1)} %pad_maximum_fusion), channel_id=1, source_target_pairs={{0,112},{8,120},{16,96},{24,104},{32,80},{40,88},{48,64},{56,72},{... | collective-permute-start | bytes 172040 | tf_op jit(solution)/shard_map/ppermute | solution.py:337
  22.4 20.2 %collective-permute-start.6 = (f32[2,56,128]{2,1,0:T(8,128)S(1)}, f32[2,56,128]{2,1,0:T(8,128)S(1)}, u32[]{:S(2)}, u32[]{:S(2)}) collective-permute-start(f32[2,56,128]{2,1,0:T(8,128)S(1)} %pad_maximum_fusion), channel_id=1, source_target_pairs={{0,96},{8,104},{16,112},{24,120},{32,64},{40,72},{48,80},{56,88},{... | collective-permute-start | bytes 172040 | tf_op jit(solution)/shard_map/ppermute | solution.py:337
  22.6 20.0 %collective-permute-start.5 = (f32[2,56,128]{2,1,0:T(8,128)S(1)}, f32[2,56,128]{2,1,0:T(8,128)S(1)}, u32[]{:S(2)}, u32[]{:S(2)}) collective-permute-start(f32[2,56,128]{2,1,0:T(8,128)S(1)} %pad_maximum_fusion), channel_id=1, source_target_pairs={{0,80},{8,88},{16,64},{24,72},{32,112},{40,120},{48,96},{56,104},{... | collective-permute-start | bytes 172040 | tf_op jit(solution)/shard_map/ppermute | solution.py:337
  25.5 17.1 %collective-permute-start.4 = (f32[2,56,128]{2,1,0:T(8,128)S(1)}, f32[2,56,128]{2,1,0:T(8,128)S(1)}, u32[]{:S(2)}, u32[]{:S(2)}) collective-permute-start(f32[2,56,128]{2,1,0:T(8,128)S(1)} %pad_maximum_fusion), channel_id=1, source_target_pairs={{0,64},{8,72},{16,80},{24,88},{32,96},{40,104},{48,112},{56,120},{... | collective-permute-start | bytes 172040 | tf_op jit(solution)/shard_map/ppermute | solution.py:337
  26.5 5.0 %collective-permute-start.1 = (f32[2,56,128]{2,1,0:T(8,128)S(1)}, f32[2,56,128]{2,1,0:T(8,128)S(1)}, u32[]{:S(2)}, u32[]{:S(2)}) collective-permute-start(f32[2,56,128]{2,1,0:T(8,128)S(1)} %pad_maximum_fusion), channel_id=1, source_target_pairs={{0,16},{8,24},{16,0},{24,8},{32,48},{40,56},{48,32},{56,40},{64,80... | collective-permute-start | bytes 172040 | tf_op jit(solution)/shard_map/ppermute | solution.py:337
  31.5 5.7 %collective-permute-start.2 = (f32[2,56,128]{2,1,0:T(8,128)S(1)}, f32[2,56,128]{2,1,0:T(8,128)S(1)}, u32[]{:S(2)}, u32[]{:S(2)}) collective-permute-start(f32[2,56,128]{2,1,0:T(8,128)S(1)} %pad_maximum_fusion), channel_id=1, source_target_pairs={{0,32},{8,40},{16,48},{24,56},{32,0},{40,8},{48,16},{56,24},{64,96... | collective-permute-start | bytes 172040 | tf_op jit(solution)/shard_map/ppermute | solution.py:337
  37.2 5.4 %collective-permute-start.3 = (f32[2,56,128]{2,1,0:T(8,128)S(1)}, f32[2,56,128]{2,1,0:T(8,128)S(1)}, u32[]{:S(2)}, u32[]{:S(2)}) collective-permute-start(f32[2,56,128]{2,1,0:T(8,128)S(1)} %pad_maximum_fusion), channel_id=1, source_target_pairs={{0,48},{8,56},{16,32},{24,40},{32,16},{40,24},{48,0},{56,8},{64,11... | collective-permute-start | bytes 172040 | tf_op jit(solution)/shard_map/ppermute | solution.py:337
  42.7 26.2 %copy-start.7 = (bf16[256,192]{0,1:T(8,128)(2,1)S(1)}, bf16[256,192]{0,1:T(8,128)(2,1)}, u32[]{:S(2)}) copy-start(bf16[256,192]{0,1:T(8,128)(2,1)} %param.13) | copy-start | bytes 294916
  42.7 26.3 %copy-start = (bf16[3072,256]{1,0:T(8,128)(2,1)S(1)}, bf16[3072,256]{1,0:T(8,128)(2,1)}, u32[]{:S(2)}) copy-start(bf16[3072,256]{1,0:T(8,128)(2,1)} %feature_ref.1) | copy-start | bytes 4718596
  65.2 14.6 %all-to-all-start.1 = ((f32[16,48,128]{2,1,0:T(8,128)}), f32[16,48,128]{2,1,0:T(8,128)S(1)}, u32[]{:S(2)}, u32[]{:S(2)}) async-start(f32[16,48,128]{2,1,0:T(8,128)} %shard_map.76), calls=%async_computation.1 | async-start | bytes 786432 | tf_op jit(solution)/shard_map/all_to_all | solution.py:353
  72.4 1.2 %copy-start.1 = (bf16[3072,256]{1,0:T(8,128)(2,1)}, bf16[3072,256]{1,0:T(8,128)(2,1)S(1)}, u32[]{:S(2)}) copy-start(bf16[3072,256]{1,0:T(8,128)(2,1)S(1)} %get-tuple-element.17.feature_ref) | copy-start | bytes 4718596
  73.6 0.8 copy-start.3
  79.8 1.4 %copy-start.2 = (bf16[3072,256]{1,0:T(8,128)(2,1)S(1)}, bf16[3072,256]{1,0:T(8,128)(2,1)}, u32[]{:S(2)}) copy-start(bf16[3072,256]{1,0:T(8,128)(2,1)} %copy-done.1) | copy-start | bytes 4718596
  82.7 1.3 %collective-permute-start.8 = (f32[48,128]{1,0:T(8,128)S(1)}, f32[48,128]{1,0:T(8,128)S(1)}, u32[]{:S(2)}, u32[]{:S(2)}) collective-permute-start(f32[48,128]{1,0:T(8,128)S(1)} %reshape.39), channel_id=1, source_target_pairs={{0,8},{8,0},{16,24},{24,16},{32,40},{40,32},{48,56},{56,48},{64,72... | collective-permute-start | bytes 73736 | tf_op jit(solution)/shard_map/ppermute | solution.py:378

commit v2 on v1

--- a/solution.py
+++ b/solution.py
@@ -244,9 +244,9 @@
 
     zeros = jnp.zeros((table_ref.shape[1] - 6 * HALF, 2 * LANES), BF16)
 
-    def evaluate(index, carry):
-        for inner in range(unroll):
-            places = [jnp.minimum((index * unroll + inner) * 2 + side, length - 1) for side in range(2)]
+    def evaluate(first, size):
+        for inner in range(size):
+            places = [jnp.minimum(first + inner * 2 + side, length - 1) for side in range(2)]
             entries = [(group_ref[place], chunk_ref[place]) for place in places]
             wave_y = jnp.concatenate([basis(entry, 1) for entry in entries], axis=1)
             high_y = wave_y.astype(BF16)
@@ -258,9 +258,18 @@
                 value = jnp.sum(inside[half * 2 * HALF : (half + 1) * 2 * HALF, :] * wave_x, axis=0, keepdims=True)
                 for side, (group, chunk) in enumerate(entries):
                     out_ref[group, pl.ds(half * chunks + chunk, 1), :] = value[:, side * LANES : (side + 1) * LANES]
+
+    def many(index, carry):
+        evaluate(index * 2 * unroll, unroll)
         return carry
 
-    lax.fori_loop(0, (length + 2 * unroll - 1) // (2 * unroll), evaluate, 0)
+    def few(index, carry):
+        evaluate(length // (2 * unroll) * 2 * unroll + index * 2 * rest, rest)
+        return carry
+
+    rest = 4
+    lax.fori_loop(0, length // (2 * unroll), many, 0)
+    lax.fori_loop(0, (length % (2 * unroll) + 2 * rest - 1) // (2 * rest), few, 0)
 
 
 def gradient_kernel(target_ref, feature_ref, net_hbm, out_ref, net_ref, sem, *, scale):

time: 107 us -> 107 us (level)
  no operation moved by 1% of the time
where the time goes in v2:
time: 107 us
  Pallas kernels  31.3 us (29%)
  starting transfers between devices  30.7 us (29%)
  blocking collectives  22.7 us (21%)
  waiting for transfers between devices  17.5 us (16%)
  local copies, waits for them, and re-layouts  4.35 us (4%)
    pallas_call x1, Pallas kernels, local(): call(functools.partial(orbital_kernel, unroll=12, each=each), jax.ShapeDt...  17.6 us
    ppermute x8, starting transfers between devices, local(): lax.ppermute(everyone, 'walk', [(k, k ^ flip) for k in range(walk_count)])  15.8 us
    all_to_all x1, blocking collectives, local(): lax.all_to_all(jnp.broadcast_to(summed, (band_count, *own.shape)), 'band'...  11.6 us
    all_to_all x1, starting transfers between devices, local(): lax.all_to_all(picked.reshape(devices, BLOCK, LANES), ('walk', 'band'), 0...  11.2 us
    all_to_all x1, blocking collectives, local(): lax.all_to_all(jnp.broadcast_to(own, (chips, *own.shape)), 'walk', 0, 0,...  11.1 us
    ppermute x8, waiting for transfers between devices, local(): lax.ppermute(everyone, 'walk', [(k, k ^ flip) for k in range(walk_count)])  10.9 us
    all_to_all x1, waiting for transfers between devices, local(): target = lax.all_to_all(values, 'walk', 0, 0, tiled=True).reshape(-1, LANES)  5.41 us
    pallas_call x1, Pallas kernels, local(): call(fold_kernel, jax.ShapeDtypeStruct((4 * HALF, 512), BF16), [pltpu.VME...  4.2 us
  transfers between devices with their start and end apart: 11, of which 6 were waited for; matrix products, arithmetic and copies ran while one was open for 0% of the time, Pallas kernels for 5%

profile of v2, /device:TPU:0, one launch (start us, length us, event | category | flops | bytes accessed | tf_op | source)
XLA Modules:
  0.0 106.7 jit_solution(13850297802573723434)
XLA Ops:
  0.0 2.6 %shard_map.73 = bf16[3072,128]{1,0:T(8,128)(2,1)} custom-call(bf16[2,1152,128]{2,1,0:T(8,128)(2,1)} %coef_hbm.1, s32[2,48]{1,0:T(2,128)} %occ_hbm.1), custom_call_target="tpu_custom_call" | custom-call | tf_op jit(solution)/shard_map/pallas_call | solution.py:323
  2.6 11.2 %all-to-all-start = ((bf16[128,24,128]{2,1,0:T(8,128)(2,1)}), bf16[128,24,128]{2,1,0:T(8,128)(2,1)S(1)}, u32[]{:S(2)}, u32[]{:S(2)}) async-start(bf16[128,24,128]{2,1,0:T(8,128)(2,1)} %bitcast), calls=%async_computation | async-start | bytes 1572864 | tf_op jit(solution)/shard_map/all_to_all | solution.py:335
  13.8 2.1 %shard_map.75 = (f32[56,128]{1,0:T(8,128)S(1)}, f32[3,1024]{1,0:T(4,128)S(1)}, f32[1,3072]{1,0:T(1,128)S(1)}) custom-call(f32[2,3072]{1,0:T(2,128)S(1)} %copy-done.4, s32[24,128]{1,0:T(8,128)S(1)} %bitcast.27), custom_call_target="tpu_custom_call" | custom-call | tf_op jit(solution)/shard_map/pallas_call | solution.py:336
  15.9 1.2 %collective-permute-done = f32[1,56,128]{2,1,0:T(8,128)S(1)} collective-permute-done((f32[1,56,128]{2,1,0:T(8,128)S(1)}, f32[1,56,128]{2,1,0:T(8,128)S(1)}, u32[]{:S(2)}, u32[]{:S(2)}) %collective-permute-start) | collective-permute-done | bytes 28704 | tf_op jit(solution)/shard_map/ppermute | solution.py:346
  17.1 5.4 %collective-permute-start.7 = (f32[2,56,128]{2,1,0:T(8,128)S(1)}, f32[2,56,128]{2,1,0:T(8,128)S(1)}, u32[]{:S(2)}, u32[]{:S(2)}) collective-permute-start(f32[2,56,128]{2,1,0:T(8,128)S(1)} %pad_maximum_fusion), channel_id=1, source_target_pairs={{0,112},{8,120},{16,96},{24,104},{32,80},{40,88},{48,64},{56,72},{... | collective-permute-start | bytes 172040 | tf_op jit(solution)/shard_map/ppermute | solution.py:346
  22.4 0.2 collective-permute-start.6
  22.6 2.9 %collective-permute-start.5 = (f32[2,56,128]{2,1,0:T(8,128)S(1)}, f32[2,56,128]{2,1,0:T(8,128)S(1)}, u32[]{:S(2)}, u32[]{:S(2)}) collective-permute-start(f32[2,56,128]{2,1,0:T(8,128)S(1)} %pad_maximum_fusion), channel_id=1, source_target_pairs={{0,80},{8,88},{16,64},{24,72},{32,112},{40,120},{48,96},{56,104},{... | collective-permute-start | bytes 172040 | tf_op jit(solution)/shard_map/ppermute | solution.py:346
  25.5 1.1 collective-permute-start.4
  26.5 1.1 %collective-permute-start.1 = (f32[2,56,128]{2,1,0:T(8,128)S(1)}, f32[2,56,128]{2,1,0:T(8,128)S(1)}, u32[]{:S(2)}, u32[]{:S(2)}) collective-permute-start(f32[2,56,128]{2,1,0:T(8,128)S(1)} %pad_maximum_fusion), channel_id=1, source_target_pairs={{0,16},{8,24},{16,0},{24,8},{32,48},{40,56},{48,32},{56,40},{64,80... | collective-permute-start | bytes 172040 | tf_op jit(solution)/shard_map/ppermute | solution.py:346
  27.6 3.9 %collective-permute-done.1 = f32[2,56,128]{2,1,0:T(8,128)S(1)} collective-permute-done((f32[2,56,128]{2,1,0:T(8,128)S(1)}, f32[2,56,128]{2,1,0:T(8,128)S(1)}, u32[]{:S(2)}, u32[]{:S(2)}) %collective-permute-start.1) | collective-permute-done | bytes 57376 | tf_op jit(solution)/shard_map/ppermute | solution.py:346
  31.5 3.0 %collective-permute-start.2 = (f32[2,56,128]{2,1,0:T(8,128)S(1)}, f32[2,56,128]{2,1,0:T(8,128)S(1)}, u32[]{:S(2)}, u32[]{:S(2)}) collective-permute-start(f32[2,56,128]{2,1,0:T(8,128)S(1)} %pad_maximum_fusion), channel_id=1, source_target_pairs={{0,32},{8,40},{16,48},{24,56},{32,0},{40,8},{48,16},{56,24},{64,96... | collective-permute-start | bytes 172040 | tf_op jit(solution)/shard_map/ppermute | solution.py:346
  34.5 2.7 %collective-permute-done.2 = f32[2,56,128]{2,1,0:T(8,128)S(1)} collective-permute-done((f32[2,56,128]{2,1,0:T(8,128)S(1)}, f32[2,56,128]{2,1,0:T(8,128)S(1)}, u32[]{:S(2)}, u32[]{:S(2)}) %collective-permute-start.2) | collective-permute-done | bytes 57376 | tf_op jit(solution)/shard_map/ppermute | solution.py:346
  37.2 2.3 %collective-permute-start.3 = (f32[2,56,128]{2,1,0:T(8,128)S(1)}, f32[2,56,128]{2,1,0:T(8,128)S(1)}, u32[]{:S(2)}, u32[]{:S(2)}) collective-permute-start(f32[2,56,128]{2,1,0:T(8,128)S(1)} %pad_maximum_fusion), channel_id=1, source_target_pairs={{0,48},{8,56},{16,32},{24,40},{32,16},{40,24},{48,0},{56,8},{64,11... | collective-permute-start | bytes 172040 | tf_op jit(solution)/shard_map/ppermute | solution.py:346
  39.4 3.1 %collective-permute-done.3 = f32[2,56,128]{2,1,0:T(8,128)S(1)} collective-permute-done((f32[2,56,128]{2,1,0:T(8,128)S(1)}, f32[2,56,128]{2,1,0:T(8,128)S(1)}, u32[]{:S(2)}, u32[]{:S(2)}) %collective-permute-start.3) | collective-permute-done | bytes 57376 | tf_op jit(solution)/shard_map/ppermute | solution.py:346
  42.6 0.0 collective-permute-done.4
  42.7 0.0 copy-start.7
  42.7 0.0 copy-start
  42.7 4.2 %shard_map.74.table_ref = bf16[320,512]{1,0:T(8,128)(2,1)S(1)} custom-call(bf16[128,24,128]{2,1,0:T(8,128)(2,1)S(1)} %all-to-all-done.recv_ref, s32[2,16,1152]{2,1,0:T(8,128)S(1)} %bitcast.22), custom_call_target="tpu_custom_call" | custom-call | tf_op jit(solution)/shard_map/pallas_call | solution.py:348
  46.9 17.6 %shard_map.76 = f32[16,48,128]{2,1,0:T(8,128)} custom-call(bf16[320,512]{1,0:T(8,128)(2,1)S(1)} %shard_map.74.table_ref, f32[16,56,128]{2,1,0:T(8,128)S(1)} %constant_dynamic-update-slice_fusion.pos_ref), custom_call_target="tpu_custom_call" | custom-call | tf_op jit(solution)/shard_map/pallas_call | solution.py:351
  64.5 3.7 %all-to-all-start.1 = ((f32[16,48,128]{2,1,0:T(8,128)}), f32[16,48,128]{2,1,0:T(8,128)S(1)}, u32[]{:S(2)}, u32[]{:S(2)}) async-start(f32[16,48,128]{2,1,0:T(8,128)} %shard_map.76), calls=%async_computation.1 | async-start | bytes 786432 | tf_op jit(solution)/shard_map/all_to_all | solution.py:362
  68.3 3.4 %shard_map.77 = (bf16[3072,256]{1,0:T(8,128)(2,1)S(1)}, f32[40,3072]{1,0:T(8,128)S(1)}) custom-call(f32[3,1024]{1,0:T(4,128)S(1)} %get-tuple-element.15.slot_ref, bf16[3072,256]{1,0:T(8,128)(2,1)S(1)} %copy-done, bf16[32,256]{1,0:T(8,128)(2,1)S(1)} %bitcast.26, f32[1,3072]{1,0:T(1,128)S(1)} %get-tuple-element.16.up_ref), custom_call_target="tpu_custom_call" | custom-call | tf_op jit(solution)/shard_map/pallas_call | solution.py:372
  71.7 1.2 %copy-done.1 = bf16[3072,256]{1,0:T(8,128)(2,1)} copy-done((bf16[3072,256]{1,0:T(8,128)(2,1)}, bf16[3072,256]{1,0:T(8,128)(2,1)S(1)}, u32[]{:S(2)}) %copy-start.1) | copy-done | bytes 1572888
  72.9 0.8 copy-done.3
  73.7 5.4 %all-to-all-done.1 = f32[16,48,128]{2,1,0:T(8,128)S(1)} async-done(((f32[16,48,128]{2,1,0:T(8,128)}), f32[16,48,128]{2,1,0:T(8,128)S(1)}, u32[]{:S(2)}, u32[]{:S(2)}) %all-to-all-start.1) | async-done | bytes 393248 | tf_op jit(solution)/shard_map/all_to_all | solution.py:362
  79.1 1.4 %copy-done.2 = bf16[3072,256]{1,0:T(8,128)(2,1)S(1)} copy-done((bf16[3072,256]{1,0:T(8,128)(2,1)S(1)}, bf16[3072,256]{1,0:T(8,128)(2,1)}, u32[]{:S(2)}) %copy-start.2) | copy-done | bytes 1572888
  80.5 1.4 %shard_map.78 = f32[32,256]{1,0:T(8,128)S(1)} custom-call(f32[768,128]{1,0:T(8,128)S(1)} %bitcast.21, bf16[3072,256]{1,0:T(8,128)(2,1)S(1)} %copy-done.2, f32[40,3072]{1,0:T(8,128)} %copy-done.3), custom_call_target="tpu_custom_call" | custom-call | tf_op jit(solution)/shard_map/pallas_call | solution.py:380
  81.9 0.1 collective-permute-start.8
  82.0 1.2 %collective-permute-done.8 = f32[48,128]{1,0:T(8,128)S(1)} collective-permute-done((f32[48,128]{1,0:T(8,128)S(1)}, f32[48,128]{1,0:T(8,128)S(1)}, u32[]{:S(2)}, u32[]{:S(2)}) %collective-permute-start.8) | collective-permute-done | bytes 24608 | tf_op jit(solution)/shard_map/ppermute | solution.py:387
  83.2 11.1 %all_to_all.20 = f32[8,48,128]{2,1,0:T(8,128)S(1)} all-to-all(f32[8,48,128]{2,1,0:T(8,128)S(1)} %broadcast_in_dim.10), channel_id=1, replica_groups={{0,16,32,48,64,80,96,112},{8,24,40,56,72,88,104,120},{1,17,33,49,65,81,..., dimensions={0} | all-to-all | bytes 393216 | tf_op jit(solution)/shard_map/all_to_all | solution.py:389
  94.4 11.6 %all_to_all.21 = f32[8,48,128]{2,1,0:T(8,128)S(1)} all-to-all(f32[8,48,128]{2,1,0:T(8,128)S(1)} %broadcast_in_dim.11), channel_id=1, replica_groups=mesh['walk'=16,'band'=8] {'band'}, dimensions={0} | all-to-all | bytes 393216 | tf_op jit(solution)/shard_map/all_to_all | solution.py:398
  106.0 0.1 reshape.40
  106.0 0.7 reshape.41
  (36 shorter events, 0.2 us)
Async XLA Ops:
  0.0 13.7 %copy-start.4 = (f32[2,3072]{1,0:T(2,128)S(1)}, f32[2,3072]{1,0:T(2,128)}, u32[]{:S(2)}) copy-start(f32[2,3072]{1,0:T(2,128)} %pos_ref) | copy-start | bytes 73732
  0.0 13.8 %copy-start.5 = (s32[3072]{0:T(1024)S(1)}, s32[3072]{0:T(1024)}, u32[]{:S(2)}) copy-start(s32[3072]{0:T(1024)} %param.10) | copy-start | bytes 36868
  0.0 15.9 %copy-start.6 = (s32[2,18432]{1,0:T(2,128)S(1)}, s32[2,18432]{1,0:T(2,128)}, u32[]{:S(2)}) copy-start(s32[2,18432]{1,0:T(2,128)} %param.9) | copy-start | bytes 442372
  2.6 40.1 %all-to-all-start = ((bf16[128,24,128]{2,1,0:T(8,128)(2,1)}), bf16[128,24,128]{2,1,0:T(8,128)(2,1)S(1)}, u32[]{:S(2)}, u32[]{:S(2)}) async-start(bf16[128,24,128]{2,1,0:T(8,128)(2,1)} %bitcast), calls=%async_computation | async-start | bytes 1572864 | tf_op jit(solution)/shard_map/all_to_all | solution.py:335
  15.8 1.2 %collective-permute-start = (f32[1,56,128]{2,1,0:T(8,128)S(1)}, f32[1,56,128]{2,1,0:T(8,128)S(1)}, u32[]{:S(2)}, u32[]{:S(2)}) collective-permute-start(f32[1,56,128]{2,1,0:T(8,128)S(1)} %bitcast.24), channel_id=1, source_target_pairs={{0,8},{8,0},{16,24},{24,16},{32,40},{40,32},{48,56},{56,48},{64,72... | collective-permute-start | bytes 86024 | tf_op jit(solution)/shard_map/ppermute | solution.py:346
  17.1 25.6 %collective-permute-start.7 = (f32[2,56,128]{2,1,0:T(8,128)S(1)}, f32[2,56,128]{2,1,0:T(8,128)S(1)}, u32[]{:S(2)}, u32[]{:S(2)}) collective-permute-start(f32[2,56,128]{2,1,0:T(8,128)S(1)} %pad_maximum_fusion), channel_id=1, source_target_pairs={{0,112},{8,120},{16,96},{24,104},{32,80},{40,88},{48,64},{56,72},{... | collective-permute-start | bytes 172040 | tf_op jit(solution)/shard_map/ppermute | solution.py:346
  22.4 20.2 %collective-permute-start.6 = (f32[2,56,128]{2,1,0:T(8,128)S(1)}, f32[2,56,128]{2,1,0:T(8,128)S(1)}, u32[]{:S(2)}, u32[]{:S(2)}) collective-permute-start(f32[2,56,128]{2,1,0:T(8,128)S(1)} %pad_maximum_fusion), channel_id=1, source_target_pairs={{0,96},{8,104},{16,112},{24,120},{32,64},{40,72},{48,80},{56,88},{... | collective-permute-start | bytes 172040 | tf_op jit(solution)/shard_map/ppermute | solution.py:346
  22.6 20.0 %collective-permute-start.5 = (f32[2,56,128]{2,1,0:T(8,128)S(1)}, f32[2,56,128]{2,1,0:T(8,128)S(1)}, u32[]{:S(2)}, u32[]{:S(2)}) collective-permute-start(f32[2,56,128]{2,1,0:T(8,128)S(1)} %pad_maximum_fusion), channel_id=1, source_target_pairs={{0,80},{8,88},{16,64},{24,72},{32,112},{40,120},{48,96},{56,104},{... | collective-permute-start | bytes 172040 | tf_op jit(solution)/shard_map/ppermute | solution.py:346
  25.5 17.1 %collective-permute-start.4 = (f32[2,56,128]{2,1,0:T(8,128)S(1)}, f32[2,56,128]{2,1,0:T(8,128)S(1)}, u32[]{:S(2)}, u32[]{:S(2)}) collective-permute-start(f32[2,56,128]{2,1,0:T(8,128)S(1)} %pad_maximum_fusion), channel_id=1, source_target_pairs={{0,64},{8,72},{16,80},{24,88},{32,96},{40,104},{48,112},{56,120},{... | collective-permute-start | bytes 172040 | tf_op jit(solution)/shard_map/ppermute | solution.py:346
  26.5 5.0 %collective-permute-start.1 = (f32[2,56,128]{2,1,0:T(8,128)S(1)}, f32[2,56,128]{2,1,0:T(8,128)S(1)}, u32[]{:S(2)}, u32[]{:S(2)}) collective-permute-start(f32[2,56,128]{2,1,0:T(8,128)S(1)} %pad_maximum_fusion), channel_id=1, source_target_pairs={{0,16},{8,24},{16,0},{24,8},{32,48},{40,56},{48,32},{56,40},{64,80... | collective-permute-start | bytes 172040 | tf_op jit(solution)/shard_map/ppermute | solution.py:346
  31.5 5.7 %collective-permute-start.2 = (f32[2,56,128]{2,1,0:T(8,128)S(1)}, f32[2,56,128]{2,1,0:T(8,128)S(1)}, u32[]{:S(2)}, u32[]{:S(2)}) collective-permute-start(f32[2,56,128]{2,1,0:T(8,128)S(1)} %pad_maximum_fusion), channel_id=1, source_target_pairs={{0,32},{8,40},{16,48},{24,56},{32,0},{40,8},{48,16},{56,24},{64,96... | collective-permute-start | bytes 172040 | tf_op jit(solution)/shard_map/ppermute | solution.py:346
  37.2 5.4 %collective-permute-start.3 = (f32[2,56,128]{2,1,0:T(8,128)S(1)}, f32[2,56,128]{2,1,0:T(8,128)S(1)}, u32[]{:S(2)}, u32[]{:S(2)}) collective-permute-start(f32[2,56,128]{2,1,0:T(8,128)S(1)} %pad_maximum_fusion), channel_id=1, source_target_pairs={{0,48},{8,56},{16,32},{24,40},{32,16},{40,24},{48,0},{56,8},{64,11... | collective-permute-start | bytes 172040 | tf_op jit(solution)/shard_map/ppermute | solution.py:346
  42.7 25.5 %copy-start.7 = (bf16[256,192]{0,1:T(8,128)(2,1)S(1)}, bf16[256,192]{0,1:T(8,128)(2,1)}, u32[]{:S(2)}) copy-start(bf16[256,192]{0,1:T(8,128)(2,1)} %param.13) | copy-start | bytes 294916
  42.7 25.6 %copy-start = (bf16[3072,256]{1,0:T(8,128)(2,1)S(1)}, bf16[3072,256]{1,0:T(8,128)(2,1)}, u32[]{:S(2)}) copy-start(bf16[3072,256]{1,0:T(8,128)(2,1)} %feature_ref.1) | copy-start | bytes 4718596
  64.5 14.6 %all-to-all-start.1 = ((f32[16,48,128]{2,1,0:T(8,128)}), f32[16,48,128]{2,1,0:T(8,128)S(1)}, u32[]{:S(2)}, u32[]{:S(2)}) async-start(f32[16,48,128]{2,1,0:T(8,128)} %shard_map.76), calls=%async_computation.1 | async-start | bytes 786432 | tf_op jit(solution)/shard_map/all_to_all | solution.py:362
  71.7 1.2 %copy-start.1 = (bf16[3072,256]{1,0:T(8,128)(2,1)}, bf16[3072,256]{1,0:T(8,128)(2,1)S(1)}, u32[]{:S(2)}) copy-start(bf16[3072,256]{1,0:T(8,128)(2,1)S(1)} %get-tuple-element.17.feature_ref) | copy-start | bytes 4718596
  72.9 0.8 copy-start.3
  79.1 1.4 %copy-start.2 = (bf16[3072,256]{1,0:T(8,128)(2,1)S(1)}, bf16[3072,256]{1,0:T(8,128)(2,1)}, u32[]{:S(2)}) copy-start(bf16[3072,256]{1,0:T(8,128)(2,1)} %copy-done.1) | copy-start | bytes 4718596
  81.9 1.3 %collective-permute-start.8 = (f32[48,128]{1,0:T(8,128)S(1)}, f32[48,128]{1,0:T(8,128)S(1)}, u32[]{:S(2)}, u32[]{:S(2)}) collective-permute-start(f32[48,128]{1,0:T(8,128)S(1)} %reshape.39), channel_id=1, source_target_pairs={{0,8},{8,0},{16,24},{24,16},{32,40},{40,32},{48,56},{56,48},{64,72... | collective-permute-start | bytes 73736 | tf_op jit(solution)/shard_map/ppermute | solution.py:387

commit v3 on v2

--- a/solution.py
+++ b/solution.py
@@ -217,12 +217,10 @@
             high = jnp.where(upper, (number + LANES - 1) // LANES, own)
             high = jnp.where(active, high, low)
 
-            def note(chunk, at):
-                group_ref[at] = group
-                chunk_ref[at] = run * own + chunk
-                return at + 1
-
-            length = lax.fori_loop(low, high, note, length)
+            for step in range(own):
+                group_ref[length + step] = group
+                chunk_ref[length + step] = run * own + low + step
+            length = length + high - low
         return length
 
     length = lax.fori_loop(0, groups, waves, 0)
@@ -354,8 +352,8 @@
         [
             pltpu.VMEM((2, walk_count, 16 * chunks, LANES), F32),
             pltpu.VMEM((2, walk_count, 2 * chunks, LANES), F32),
-            pltpu.SMEM((walk_count * chunks,), jnp.int32),
-            pltpu.SMEM((walk_count * chunks,), jnp.int32),
+            pltpu.SMEM((walk_count * chunks + RUN // LANES,), jnp.int32),
+            pltpu.SMEM((walk_count * chunks + RUN // LANES,), jnp.int32),
         ],
         mebibytes=24,
     )(table, everyone)

time: 107 us -> 105 us (0.981)
  Pallas kernels: 31.3 us -> 28.9 us
    pallas_call x1, Pallas kernels: 17.6 us -> 15.2 us  [local(): call(functools.partial(orbital_kernel, unroll=12, each=each), jax.ShapeDt...]
where the time goes in v3:
time: 105 us; the launch traced here: 104 us
  starting transfers between devices  30.7 us (29%)
  Pallas kernels  28.9 us (28%)
  blocking collectives  22.7 us (22%)
  waiting for transfers between devices  17.5 us (17%)
  local copies, waits for them, and re-layouts  4.35 us (4%)
    ppermute x8, starting transfers between devices, local(): lax.ppermute(everyone, 'walk', [(k, k ^ flip) for k in range(walk_count)])  15.8 us
    pallas_call x1, Pallas kernels, local(): call(functools.partial(orbital_kernel, unroll=12, each=each), jax.ShapeDt...  15.2 us
    all_to_all x1, blocking collectives, local(): lax.all_to_all(jnp.broadcast_to(summed, (band_count, *own.shape)), 'band'...  11.6 us
    all_to_all x1, starting transfers between devices, local(): lax.all_to_all(picked.reshape(devices, BLOCK, LANES), ('walk', 'band'), 0...  11.2 us
    all_to_all x1, blocking collectives, local(): lax.all_to_all(jnp.broadcast_to(own, (chips, *own.shape)), 'walk', 0, 0,...  11.1 us
    ppermute x8, waiting for transfers between devices, local(): lax.ppermute(everyone, 'walk', [(k, k ^ flip) for k in range(walk_count)])  10.9 us
    all_to_all x1, waiting for transfers between devices, local(): target = lax.all_to_all(values, 'walk', 0, 0, tiled=True).reshape(-1, LANES)  5.41 us
    pallas_call x1, Pallas kernels, local(): call(fold_kernel, jax.ShapeDtypeStruct((4 * HALF, 512), BF16), [pltpu.VME...  4.2 us
  transfers between devices with their start and end apart: 11, of which 6 were waited for; matrix products, arithmetic and copies ran while one was open for 0% of the time, Pallas kernels for 5%

profile of v3, /device:TPU:0, one launch (start us, length us, event | category | flops | bytes accessed | tf_op | source)
XLA Modules:
  0.0 104.4 jit_solution(5533961628823809894)
XLA Ops:
  0.0 2.6 %shard_map.73 = bf16[3072,128]{1,0:T(8,128)(2,1)} custom-call(bf16[2,1152,128]{2,1,0:T(8,128)(2,1)} %coef_hbm.1, s32[2,48]{1,0:T(2,128)} %occ_hbm.1), custom_call_target="tpu_custom_call" | custom-call | tf_op jit(solution)/shard_map/pallas_call | solution.py:321
  2.6 11.2 %all-to-all-start = ((bf16[128,24,128]{2,1,0:T(8,128)(2,1)}), bf16[128,24,128]{2,1,0:T(8,128)(2,1)S(1)}, u32[]{:S(2)}, u32[]{:S(2)}) async-start(bf16[128,24,128]{2,1,0:T(8,128)(2,1)} %bitcast), calls=%async_computation | async-start | bytes 1572864 | tf_op jit(solution)/shard_map/all_to_all | solution.py:333
  13.8 2.1 %shard_map.75 = (f32[56,128]{1,0:T(8,128)S(1)}, f32[3,1024]{1,0:T(4,128)S(1)}, f32[1,3072]{1,0:T(1,128)S(1)}) custom-call(f32[2,3072]{1,0:T(2,128)S(1)} %copy-done.4, s32[24,128]{1,0:T(8,128)S(1)} %bitcast.27), custom_call_target="tpu_custom_call" | custom-call | tf_op jit(solution)/shard_map/pallas_call | solution.py:334
  15.9 1.2 %collective-permute-done = f32[1,56,128]{2,1,0:T(8,128)S(1)} collective-permute-done((f32[1,56,128]{2,1,0:T(8,128)S(1)}, f32[1,56,128]{2,1,0:T(8,128)S(1)}, u32[]{:S(2)}, u32[]{:S(2)}) %collective-permute-start) | collective-permute-done | bytes 28704 | tf_op jit(solution)/shard_map/ppermute | solution.py:344
  17.1 5.4 %collective-permute-start.7 = (f32[2,56,128]{2,1,0:T(8,128)S(1)}, f32[2,56,128]{2,1,0:T(8,128)S(1)}, u32[]{:S(2)}, u32[]{:S(2)}) collective-permute-start(f32[2,56,128]{2,1,0:T(8,128)S(1)} %pad_maximum_fusion), channel_id=1, source_target_pairs={{0,112},{8,120},{16,96},{24,104},{32,80},{40,88},{48,64},{56,72},{... | collective-permute-start | bytes 172040 | tf_op jit(solution)/shard_map/ppermute | solution.py:344
  22.4 0.2 collective-permute-start.6
  22.6 2.9 %collective-permute-start.5 = (f32[2,56,128]{2,1,0:T(8,128)S(1)}, f32[2,56,128]{2,1,0:T(8,128)S(1)}, u32[]{:S(2)}, u32[]{:S(2)}) collective-permute-start(f32[2,56,128]{2,1,0:T(8,128)S(1)} %pad_maximum_fusion), channel_id=1, source_target_pairs={{0,80},{8,88},{16,64},{24,72},{32,112},{40,120},{48,96},{56,104},{... | collective-permute-start | bytes 172040 | tf_op jit(solution)/shard_map/ppermute | solution.py:344
  25.5 1.1 %collective-permute-start.4 = (f32[2,56,128]{2,1,0:T(8,128)S(1)}, f32[2,56,128]{2,1,0:T(8,128)S(1)}, u32[]{:S(2)}, u32[]{:S(2)}) collective-permute-start(f32[2,56,128]{2,1,0:T(8,128)S(1)} %pad_maximum_fusion), channel_id=1, source_target_pairs={{0,64},{8,72},{16,80},{24,88},{32,96},{40,104},{48,112},{56,120},{... | collective-permute-start | bytes 172040 | tf_op jit(solution)/shard_map/ppermute | solution.py:344
  26.5 1.1 %collective-permute-start.1 = (f32[2,56,128]{2,1,0:T(8,128)S(1)}, f32[2,56,128]{2,1,0:T(8,128)S(1)}, u32[]{:S(2)}, u32[]{:S(2)}) collective-permute-start(f32[2,56,128]{2,1,0:T(8,128)S(1)} %pad_maximum_fusion), channel_id=1, source_target_pairs={{0,16},{8,24},{16,0},{24,8},{32,48},{40,56},{48,32},{56,40},{64,80... | collective-permute-start | bytes 172040 | tf_op jit(solution)/shard_map/ppermute | solution.py:344
  27.6 3.9 %collective-permute-done.1 = f32[2,56,128]{2,1,0:T(8,128)S(1)} collective-permute-done((f32[2,56,128]{2,1,0:T(8,128)S(1)}, f32[2,56,128]{2,1,0:T(8,128)S(1)}, u32[]{:S(2)}, u32[]{:S(2)}) %collective-permute-start.1) | collective-permute-done | bytes 57376 | tf_op jit(solution)/shard_map/ppermute | solution.py:344
  31.5 3.0 %collective-permute-start.2 = (f32[2,56,128]{2,1,0:T(8,128)S(1)}, f32[2,56,128]{2,1,0:T(8,128)S(1)}, u32[]{:S(2)}, u32[]{:S(2)}) collective-permute-start(f32[2,56,128]{2,1,0:T(8,128)S(1)} %pad_maximum_fusion), channel_id=1, source_target_pairs={{0,32},{8,40},{16,48},{24,56},{32,0},{40,8},{48,16},{56,24},{64,96... | collective-permute-start | bytes 172040 | tf_op jit(solution)/shard_map/ppermute | solution.py:344
  34.5 2.7 %collective-permute-done.2 = f32[2,56,128]{2,1,0:T(8,128)S(1)} collective-permute-done((f32[2,56,128]{2,1,0:T(8,128)S(1)}, f32[2,56,128]{2,1,0:T(8,128)S(1)}, u32[]{:S(2)}, u32[]{:S(2)}) %collective-permute-start.2) | collective-permute-done | bytes 57376 | tf_op jit(solution)/shard_map/ppermute | solution.py:344
  37.2 2.3 %collective-permute-start.3 = (f32[2,56,128]{2,1,0:T(8,128)S(1)}, f32[2,56,128]{2,1,0:T(8,128)S(1)}, u32[]{:S(2)}, u32[]{:S(2)}) collective-permute-start(f32[2,56,128]{2,1,0:T(8,128)S(1)} %pad_maximum_fusion), channel_id=1, source_target_pairs={{0,48},{8,56},{16,32},{24,40},{32,16},{40,24},{48,0},{56,8},{64,11... | collective-permute-start | bytes 172040 | tf_op jit(solution)/shard_map/ppermute | solution.py:344
  39.4 3.1 %collective-permute-done.3 = f32[2,56,128]{2,1,0:T(8,128)S(1)} collective-permute-done((f32[2,56,128]{2,1,0:T(8,128)S(1)}, f32[2,56,128]{2,1,0:T(8,128)S(1)}, u32[]{:S(2)}, u32[]{:S(2)}) %collective-permute-start.3) | collective-permute-done | bytes 57376 | tf_op jit(solution)/shard_map/ppermute | solution.py:344
  42.6 0.0 collective-permute-done.4
  42.7 0.0 copy-start.7
  42.7 0.0 copy-start
  42.7 4.2 %shard_map.74.table_ref = bf16[320,512]{1,0:T(8,128)(2,1)S(1)} custom-call(bf16[128,24,128]{2,1,0:T(8,128)(2,1)S(1)} %all-to-all-done.recv_ref, s32[2,16,1152]{2,1,0:T(8,128)S(1)} %bitcast.22), custom_call_target="tpu_custom_call" | custom-call | tf_op jit(solution)/shard_map/pallas_call | solution.py:346
  46.9 15.2 %shard_map.76 = f32[16,48,128]{2,1,0:T(8,128)} custom-call(bf16[320,512]{1,0:T(8,128)(2,1)S(1)} %shard_map.74.table_ref, f32[16,56,128]{2,1,0:T(8,128)S(1)} %constant_dynamic-update-slice_fusion.pos_ref), custom_call_target="tpu_custom_call" | custom-call | tf_op jit(solution)/shard_map/pallas_call | solution.py:349
  62.2 3.7 %all-to-all-start.1 = ((f32[16,48,128]{2,1,0:T(8,128)}), f32[16,48,128]{2,1,0:T(8,128)S(1)}, u32[]{:S(2)}, u32[]{:S(2)}) async-start(f32[16,48,128]{2,1,0:T(8,128)} %shard_map.76), calls=%async_computation.1 | async-start | bytes 786432 | tf_op jit(solution)/shard_map/all_to_all | solution.py:360
  66.0 3.4 %shard_map.77 = (bf16[3072,256]{1,0:T(8,128)(2,1)S(1)}, f32[40,3072]{1,0:T(8,128)S(1)}) custom-call(f32[3,1024]{1,0:T(4,128)S(1)} %get-tuple-element.15.slot_ref, bf16[3072,256]{1,0:T(8,128)(2,1)S(1)} %copy-done, bf16[32,256]{1,0:T(8,128)(2,1)S(1)} %bitcast.26, f32[1,3072]{1,0:T(1,128)S(1)} %get-tuple-element.16.up_ref), custom_call_target="tpu_custom_call" | custom-call | tf_op jit(solution)/shard_map/pallas_call | solution.py:370
  69.4 1.2 %copy-done.1 = bf16[3072,256]{1,0:T(8,128)(2,1)} copy-done((bf16[3072,256]{1,0:T(8,128)(2,1)}, bf16[3072,256]{1,0:T(8,128)(2,1)S(1)}, u32[]{:S(2)}) %copy-start.1) | copy-done | bytes 1572888
  70.6 0.8 copy-done.3
  71.4 5.4 %all-to-all-done.1 = f32[16,48,128]{2,1,0:T(8,128)S(1)} async-done(((f32[16,48,128]{2,1,0:T(8,128)}), f32[16,48,128]{2,1,0:T(8,128)S(1)}, u32[]{:S(2)}, u32[]{:S(2)}) %all-to-all-start.1) | async-done | bytes 393248 | tf_op jit(solution)/shard_map/all_to_all | solution.py:360
  76.8 1.4 %copy-done.2 = bf16[3072,256]{1,0:T(8,128)(2,1)S(1)} copy-done((bf16[3072,256]{1,0:T(8,128)(2,1)S(1)}, bf16[3072,256]{1,0:T(8,128)(2,1)}, u32[]{:S(2)}) %copy-start.2) | copy-done | bytes 1572888
  78.2 1.4 %shard_map.78 = f32[32,256]{1,0:T(8,128)S(1)} custom-call(f32[768,128]{1,0:T(8,128)S(1)} %bitcast.21, bf16[3072,256]{1,0:T(8,128)(2,1)S(1)} %copy-done.2, f32[40,3072]{1,0:T(8,128)} %copy-done.3), custom_call_target="tpu_custom_call" | custom-call | tf_op jit(solution)/shard_map/pallas_call | solution.py:378
  79.6 0.1 collective-permute-start.8
  79.7 1.2 %collective-permute-done.8 = f32[48,128]{1,0:T(8,128)S(1)} collective-permute-done((f32[48,128]{1,0:T(8,128)S(1)}, f32[48,128]{1,0:T(8,128)S(1)}, u32[]{:S(2)}, u32[]{:S(2)}) %collective-permute-start.8) | collective-permute-done | bytes 24608 | tf_op jit(solution)/shard_map/ppermute | solution.py:385
  80.9 11.1 %all_to_all.20 = f32[8,48,128]{2,1,0:T(8,128)S(1)} all-to-all(f32[8,48,128]{2,1,0:T(8,128)S(1)} %broadcast_in_dim.10), channel_id=1, replica_groups={{0,16,32,48,64,80,96,112},{8,24,40,56,72,88,104,120},{1,17,33,49,65,81,..., dimensions={0} | all-to-all | bytes 393216 | tf_op jit(solution)/shard_map/all_to_all | solution.py:387
  92.1 11.6 %all_to_all.21 = f32[8,48,128]{2,1,0:T(8,128)S(1)} all-to-all(f32[8,48,128]{2,1,0:T(8,128)S(1)} %broadcast_in_dim.11), channel_id=1, replica_groups=mesh['walk'=16,'band'=8] {'band'}, dimensions={0} | all-to-all | bytes 393216 | tf_op jit(solution)/shard_map/all_to_all | solution.py:396
  103.7 0.1 reshape.40
  103.7 0.7 reshape.41
  (36 shorter events, 0.2 us)
Async XLA Ops:
  0.0 13.7 %copy-start.4 = (f32[2,3072]{1,0:T(2,128)S(1)}, f32[2,3072]{1,0:T(2,128)}, u32[]{:S(2)}) copy-start(f32[2,3072]{1,0:T(2,128)} %pos_ref) | copy-start | bytes 73732
  0.0 13.8 %copy-start.5 = (s32[3072]{0:T(1024)S(1)}, s32[3072]{0:T(1024)}, u32[]{:S(2)}) copy-start(s32[3072]{0:T(1024)} %param.10) | copy-start | bytes 36868
  0.0 15.9 %copy-start.6 = (s32[2,18432]{1,0:T(2,128)S(1)}, s32[2,18432]{1,0:T(2,128)}, u32[]{:S(2)}) copy-start(s32[2,18432]{1,0:T(2,128)} %param.9) | copy-start | bytes 442372
  2.6 40.1 %all-to-all-start = ((bf16[128,24,128]{2,1,0:T(8,128)(2,1)}), bf16[128,24,128]{2,1,0:T(8,128)(2,1)S(1)}, u32[]{:S(2)}, u32[]{:S(2)}) async-start(bf16[128,24,128]{2,1,0:T(8,128)(2,1)} %bitcast), calls=%async_computation | async-start | bytes 1572864 | tf_op jit(solution)/shard_map/all_to_all | solution.py:333
  15.8 1.2 %collective-permute-start = (f32[1,56,128]{2,1,0:T(8,128)S(1)}, f32[1,56,128]{2,1,0:T(8,128)S(1)}, u32[]{:S(2)}, u32[]{:S(2)}) collective-permute-start(f32[1,56,128]{2,1,0:T(8,128)S(1)} %bitcast.24), channel_id=1, source_target_pairs={{0,8},{8,0},{16,24},{24,16},{32,40},{40,32},{48,56},{56,48},{64,72... | collective-permute-start | bytes 86024 | tf_op jit(solution)/shard_map/ppermute | solution.py:344
  17.1 25.6 %collective-permute-start.7 = (f32[2,56,128]{2,1,0:T(8,128)S(1)}, f32[2,56,128]{2,1,0:T(8,128)S(1)}, u32[]{:S(2)}, u32[]{:S(2)}) collective-permute-start(f32[2,56,128]{2,1,0:T(8,128)S(1)} %pad_maximum_fusion), channel_id=1, source_target_pairs={{0,112},{8,120},{16,96},{24,104},{32,80},{40,88},{48,64},{56,72},{... | collective-permute-start | bytes 172040 | tf_op jit(solution)/shard_map/ppermute | solution.py:344
  22.4 20.2 %collective-permute-start.6 = (f32[2,56,128]{2,1,0:T(8,128)S(1)}, f32[2,56,128]{2,1,0:T(8,128)S(1)}, u32[]{:S(2)}, u32[]{:S(2)}) collective-permute-start(f32[2,56,128]{2,1,0:T(8,128)S(1)} %pad_maximum_fusion), channel_id=1, source_target_pairs={{0,96},{8,104},{16,112},{24,120},{32,64},{40,72},{48,80},{56,88},{... | collective-permute-start | bytes 172040 | tf_op jit(solution)/shard_map/ppermute | solution.py:344
  22.6 20.0 %collective-permute-start.5 = (f32[2,56,128]{2,1,0:T(8,128)S(1)}, f32[2,56,128]{2,1,0:T(8,128)S(1)}, u32[]{:S(2)}, u32[]{:S(2)}) collective-permute-start(f32[2,56,128]{2,1,0:T(8,128)S(1)} %pad_maximum_fusion), channel_id=1, source_target_pairs={{0,80},{8,88},{16,64},{24,72},{32,112},{40,120},{48,96},{56,104},{... | collective-permute-start | bytes 172040 | tf_op jit(solution)/shard_map/ppermute | solution.py:344
  25.5 17.1 %collective-permute-start.4 = (f32[2,56,128]{2,1,0:T(8,128)S(1)}, f32[2,56,128]{2,1,0:T(8,128)S(1)}, u32[]{:S(2)}, u32[]{:S(2)}) collective-permute-start(f32[2,56,128]{2,1,0:T(8,128)S(1)} %pad_maximum_fusion), channel_id=1, source_target_pairs={{0,64},{8,72},{16,80},{24,88},{32,96},{40,104},{48,112},{56,120},{... | collective-permute-start | bytes 172040 | tf_op jit(solution)/shard_map/ppermute | solution.py:344
  26.5 5.0 %collective-permute-start.1 = (f32[2,56,128]{2,1,0:T(8,128)S(1)}, f32[2,56,128]{2,1,0:T(8,128)S(1)}, u32[]{:S(2)}, u32[]{:S(2)}) collective-permute-start(f32[2,56,128]{2,1,0:T(8,128)S(1)} %pad_maximum_fusion), channel_id=1, source_target_pairs={{0,16},{8,24},{16,0},{24,8},{32,48},{40,56},{48,32},{56,40},{64,80... | collective-permute-start | bytes 172040 | tf_op jit(solution)/shard_map/ppermute | solution.py:344
  31.5 5.7 %collective-permute-start.2 = (f32[2,56,128]{2,1,0:T(8,128)S(1)}, f32[2,56,128]{2,1,0:T(8,128)S(1)}, u32[]{:S(2)}, u32[]{:S(2)}) collective-permute-start(f32[2,56,128]{2,1,0:T(8,128)S(1)} %pad_maximum_fusion), channel_id=1, source_target_pairs={{0,32},{8,40},{16,48},{24,56},{32,0},{40,8},{48,16},{56,24},{64,96... | collective-permute-start | bytes 172040 | tf_op jit(solution)/shard_map/ppermute | solution.py:344
  37.2 5.4 %collective-permute-start.3 = (f32[2,56,128]{2,1,0:T(8,128)S(1)}, f32[2,56,128]{2,1,0:T(8,128)S(1)}, u32[]{:S(2)}, u32[]{:S(2)}) collective-permute-start(f32[2,56,128]{2,1,0:T(8,128)S(1)} %pad_maximum_fusion), channel_id=1, source_target_pairs={{0,48},{8,56},{16,32},{24,40},{32,16},{40,24},{48,0},{56,8},{64,11... | collective-permute-start | bytes 172040 | tf_op jit(solution)/shard_map/ppermute | solution.py:344
  42.7 23.2 %copy-start.7 = (bf16[256,192]{0,1:T(8,128)(2,1)S(1)}, bf16[256,192]{0,1:T(8,128)(2,1)}, u32[]{:S(2)}) copy-start(bf16[256,192]{0,1:T(8,128)(2,1)} %param.13) | copy-start | bytes 294916
  42.7 23.3 %copy-start = (bf16[3072,256]{1,0:T(8,128)(2,1)S(1)}, bf16[3072,256]{1,0:T(8,128)(2,1)}, u32[]{:S(2)}) copy-start(bf16[3072,256]{1,0:T(8,128)(2,1)} %feature_ref.1) | copy-start | bytes 4718596
  62.2 14.6 %all-to-all-start.1 = ((f32[16,48,128]{2,1,0:T(8,128)}), f32[16,48,128]{2,1,0:T(8,128)S(1)}, u32[]{:S(2)}, u32[]{:S(2)}) async-start(f32[16,48,128]{2,1,0:T(8,128)} %shard_map.76), calls=%async_computation.1 | async-start | bytes 786432 | tf_op jit(solution)/shard_map/all_to_all | solution.py:360
  69.4 1.2 %copy-start.1 = (bf16[3072,256]{1,0:T(8,128)(2,1)}, bf16[3072,256]{1,0:T(8,128)(2,1)S(1)}, u32[]{:S(2)}) copy-start(bf16[3072,256]{1,0:T(8,128)(2,1)S(1)} %get-tuple-element.17.feature_ref) | copy-start | bytes 4718596
  70.5 0.8 copy-start.3
  76.8 1.4 %copy-start.2 = (bf16[3072,256]{1,0:T(8,128)(2,1)S(1)}, bf16[3072,256]{1,0:T(8,128)(2,1)}, u32[]{:S(2)}) copy-start(bf16[3072,256]{1,0:T(8,128)(2,1)} %copy-done.1) | copy-start | bytes 4718596
  79.6 1.3 %collective-permute-start.8 = (f32[48,128]{1,0:T(8,128)S(1)}, f32[48,128]{1,0:T(8,128)S(1)}, u32[]{:S(2)}, u32[]{:S(2)}) collective-permute-start(f32[48,128]{1,0:T(8,128)S(1)} %reshape.39), channel_id=1, source_target_pairs={{0,8},{8,0},{16,24},{24,16},{32,40},{40,32},{48,56},{56,48},{64,72... | collective-permute-start | bytes 73736 | tf_op jit(solution)/shard_map/ppermute | solution.py:385

commit v4 on v3

--- a/solution.py
+++ b/solution.py
@@ -189,7 +189,7 @@
     table_ref[...] = jnp.concatenate([high, high, low, pad], axis=1).astype(BF16)
 
 
-def orbital_kernel(table_ref, pos_ref, out_ref, wave_ref, eight_ref, group_ref, chunk_ref, *, unroll, each):
+def orbital_kernel(table_ref, pos_ref, out_ref, wave_ref, eight_ref, list_ref, *, unroll, each):
     groups = out_ref.shape[0]
     chunks = out_ref.shape[1] // 2
     own = RUN // LANES
@@ -218,12 +218,11 @@
             high = jnp.where(active, high, low)
 
             for step in range(own):
-                group_ref[length + step] = group
-                chunk_ref[length + step] = run * own + low + step
+                list_ref[length + step] = group * LANES + run * own + low + step
             length = length + high - low
         return length
 
-    length = lax.fori_loop(0, groups, waves, 0)
+    length = lax.fori_loop(0, groups, waves, 0, unroll=2)
 
     def basis(entry, axis):
         group, chunk = entry
@@ -245,7 +244,7 @@
     def evaluate(first, size):
         for inner in range(size):
             places = [jnp.minimum(first + inner * 2 + side, length - 1) for side in range(2)]
-            entries = [(group_ref[place], chunk_ref[place]) for place in places]
+            entries = [(list_ref[place] >> 7, list_ref[place] & (LANES - 1)) for place in places]
             wave_y = jnp.concatenate([basis(entry, 1) for entry in entries], axis=1)
             high_y = wave_y.astype(BF16)
             low_y = (wave_y - high_y.astype(F32)).astype(BF16)
@@ -353,7 +352,6 @@
             pltpu.VMEM((2, walk_count, 16 * chunks, LANES), F32),
             pltpu.VMEM((2, walk_count, 2 * chunks, LANES), F32),
             pltpu.SMEM((walk_count * chunks + RUN // LANES,), jnp.int32),
-            pltpu.SMEM((walk_count * chunks + RUN // LANES,), jnp.int32),
         ],
         mebibytes=24,
     )(table, everyone)

time: 105 us -> 104 us (level)
  no operation moved by 1% of the time
where the time goes in v4:
time: 104 us
  starting transfers between devices  30.7 us (30%)
  Pallas kernels  28.4 us (27%)
  blocking collectives  22.7 us (22%)
  waiting for transfers between devices  17.5 us (17%)
  local copies, waits for them, and re-layouts  4.35 us (4%)
    ppermute x8, starting transfers between devices, local(): lax.ppermute(everyone, 'walk', [(k, k ^ flip) for k in range(walk_count)])  15.8 us
    pallas_call x1, Pallas kernels, local(): call(functools.partial(orbital_kernel, unroll=12, each=each), jax.ShapeDt...  14.7 us
    all_to_all x1, blocking collectives, local(): lax.all_to_all(jnp.broadcast_to(summed, (band_count, *own.shape)), 'band'...  11.6 us
    all_to_all x1, starting transfers between devices, local(): lax.all_to_all(picked.reshape(devices, BLOCK, LANES), ('walk', 'band'), 0...  11.2 us
    all_to_all x1, blocking collectives, local(): lax.all_to_all(jnp.broadcast_to(own, (chips, *own.shape)), 'walk', 0, 0,...  11.1 us
    ppermute x8, waiting for transfers between devices, local(): lax.ppermute(everyone, 'walk', [(k, k ^ flip) for k in range(walk_count)])  10.9 us
    all_to_all x1, waiting for transfers between devices, local(): target = lax.all_to_all(values, 'walk', 0, 0, tiled=True).reshape(-1, LANES)  5.41 us
    pallas_call x1, Pallas kernels, local(): call(fold_kernel, jax.ShapeDtypeStruct((4 * HALF, 512), BF16), [pltpu.VME...  4.2 us
  transfers between devices with their start and end apart: 11, of which 6 were waited for; matrix products, arithmetic and copies ran while one was open for 0% of the time, Pallas kernels for 5%

profile of v4, /device:TPU:0, one launch (start us, length us, event | category | flops | bytes accessed | tf_op | source)
XLA Modules:
  0.0 103.9 jit_solution(2710788983131423451)
XLA Ops:
  0.0 2.6 %shard_map.73 = bf16[3072,128]{1,0:T(8,128)(2,1)} custom-call(bf16[2,1152,128]{2,1,0:T(8,128)(2,1)} %coef_hbm.1, s32[2,48]{1,0:T(2,128)} %occ_hbm.1), custom_call_target="tpu_custom_call" | custom-call | tf_op jit(solution)/shard_map/pallas_call | solution.py:320
  2.6 11.2 %all-to-all-start = ((bf16[128,24,128]{2,1,0:T(8,128)(2,1)}), bf16[128,24,128]{2,1,0:T(8,128)(2,1)S(1)}, u32[]{:S(2)}, u32[]{:S(2)}) async-start(bf16[128,24,128]{2,1,0:T(8,128)(2,1)} %bitcast), calls=%async_computation | async-start | bytes 1572864 | tf_op jit(solution)/shard_map/all_to_all | solution.py:332
  13.8 2.1 %shard_map.75 = (f32[56,128]{1,0:T(8,128)S(1)}, f32[3,1024]{1,0:T(4,128)S(1)}, f32[1,3072]{1,0:T(1,128)S(1)}) custom-call(f32[2,3072]{1,0:T(2,128)S(1)} %copy-done.4, s32[24,128]{1,0:T(8,128)S(1)} %bitcast.27), custom_call_target="tpu_custom_call" | custom-call | tf_op jit(solution)/shard_map/pallas_call | solution.py:333
  15.9 1.2 %collective-permute-done = f32[1,56,128]{2,1,0:T(8,128)S(1)} collective-permute-done((f32[1,56,128]{2,1,0:T(8,128)S(1)}, f32[1,56,128]{2,1,0:T(8,128)S(1)}, u32[]{:S(2)}, u32[]{:S(2)}) %collective-permute-start) | collective-permute-done | bytes 28704 | tf_op jit(solution)/shard_map/ppermute | solution.py:343
  17.1 5.4 %collective-permute-start.7 = (f32[2,56,128]{2,1,0:T(8,128)S(1)}, f32[2,56,128]{2,1,0:T(8,128)S(1)}, u32[]{:S(2)}, u32[]{:S(2)}) collective-permute-start(f32[2,56,128]{2,1,0:T(8,128)S(1)} %pad_maximum_fusion), channel_id=1, source_target_pairs={{0,112},{8,120},{16,96},{24,104},{32,80},{40,88},{48,64},{56,72},{... | collective-permute-start | bytes 172040 | tf_op jit(solution)/shard_map/ppermute | solution.py:343
  22.4 0.2 collective-permute-start.6
  22.6 2.9 %collective-permute-start.5 = (f32[2,56,128]{2,1,0:T(8,128)S(1)}, f32[2,56,128]{2,1,0:T(8,128)S(1)}, u32[]{:S(2)}, u32[]{:S(2)}) collective-permute-start(f32[2,56,128]{2,1,0:T(8,128)S(1)} %pad_maximum_fusion), channel_id=1, source_target_pairs={{0,80},{8,88},{16,64},{24,72},{32,112},{40,120},{48,96},{56,104},{... | collective-permute-start | bytes 172040 | tf_op jit(solution)/shard_map/ppermute | solution.py:343
  25.5 1.1 %collective-permute-start.4 = (f32[2,56,128]{2,1,0:T(8,128)S(1)}, f32[2,56,128]{2,1,0:T(8,128)S(1)}, u32[]{:S(2)}, u32[]{:S(2)}) collective-permute-start(f32[2,56,128]{2,1,0:T(8,128)S(1)} %pad_maximum_fusion), channel_id=1, source_target_pairs={{0,64},{8,72},{16,80},{24,88},{32,96},{40,104},{48,112},{56,120},{... | collective-permute-start | bytes 172040 | tf_op jit(solution)/shard_map/ppermute | solution.py:343
  26.5 1.1 %collective-permute-start.1 = (f32[2,56,128]{2,1,0:T(8,128)S(1)}, f32[2,56,128]{2,1,0:T(8,128)S(1)}, u32[]{:S(2)}, u32[]{:S(2)}) collective-permute-start(f32[2,56,128]{2,1,0:T(8,128)S(1)} %pad_maximum_fusion), channel_id=1, source_target_pairs={{0,16},{8,24},{16,0},{24,8},{32,48},{40,56},{48,32},{56,40},{64,80... | collective-permute-start | bytes 172040 | tf_op jit(solution)/shard_map/ppermute | solution.py:343
  27.6 3.9 %collective-permute-done.1 = f32[2,56,128]{2,1,0:T(8,128)S(1)} collective-permute-done((f32[2,56,128]{2,1,0:T(8,128)S(1)}, f32[2,56,128]{2,1,0:T(8,128)S(1)}, u32[]{:S(2)}, u32[]{:S(2)}) %collective-permute-start.1) | collective-permute-done | bytes 57376 | tf_op jit(solution)/shard_map/ppermute | solution.py:343
  31.5 3.0 %collective-permute-start.2 = (f32[2,56,128]{2,1,0:T(8,128)S(1)}, f32[2,56,128]{2,1,0:T(8,128)S(1)}, u32[]{:S(2)}, u32[]{:S(2)}) collective-permute-start(f32[2,56,128]{2,1,0:T(8,128)S(1)} %pad_maximum_fusion), channel_id=1, source_target_pairs={{0,32},{8,40},{16,48},{24,56},{32,0},{40,8},{48,16},{56,24},{64,96... | collective-permute-start | bytes 172040 | tf_op jit(solution)/shard_map/ppermute | solution.py:343
  34.5 2.7 %collective-permute-done.2 = f32[2,56,128]{2,1,0:T(8,128)S(1)} collective-permute-done((f32[2,56,128]{2,1,0:T(8,128)S(1)}, f32[2,56,128]{2,1,0:T(8,128)S(1)}, u32[]{:S(2)}, u32[]{:S(2)}) %collective-permute-start.2) | collective-permute-done | bytes 57376 | tf_op jit(solution)/shard_map/ppermute | solution.py:343
  37.2 2.3 %collective-permute-start.3 = (f32[2,56,128]{2,1,0:T(8,128)S(1)}, f32[2,56,128]{2,1,0:T(8,128)S(1)}, u32[]{:S(2)}, u32[]{:S(2)}) collective-permute-start(f32[2,56,128]{2,1,0:T(8,128)S(1)} %pad_maximum_fusion), channel_id=1, source_target_pairs={{0,48},{8,56},{16,32},{24,40},{32,16},{40,24},{48,0},{56,8},{64,11... | collective-permute-start | bytes 172040 | tf_op jit(solution)/shard_map/ppermute | solution.py:343
  39.4 3.1 %collective-permute-done.3 = f32[2,56,128]{2,1,0:T(8,128)S(1)} collective-permute-done((f32[2,56,128]{2,1,0:T(8,128)S(1)}, f32[2,56,128]{2,1,0:T(8,128)S(1)}, u32[]{:S(2)}, u32[]{:S(2)}) %collective-permute-start.3) | collective-permute-done | bytes 57376 | tf_op jit(solution)/shard_map/ppermute | solution.py:343
  42.6 0.0 collective-permute-done.4
  42.7 0.0 copy-start.7
  42.7 0.0 copy-start
  42.7 4.2 %shard_map.74.table_ref = bf16[320,512]{1,0:T(8,128)(2,1)S(1)} custom-call(bf16[128,24,128]{2,1,0:T(8,128)(2,1)S(1)} %all-to-all-done.recv_ref, s32[2,16,1152]{2,1,0:T(8,128)S(1)} %bitcast.22), custom_call_target="tpu_custom_call" | custom-call | tf_op jit(solution)/shard_map/pallas_call | solution.py:345
  46.9 14.7 %shard_map.76 = f32[16,48,128]{2,1,0:T(8,128)} custom-call(bf16[320,512]{1,0:T(8,128)(2,1)S(1)} %shard_map.74.table_ref, f32[16,56,128]{2,1,0:T(8,128)S(1)} %constant_dynamic-update-slice_fusion.pos_ref), custom_call_target="tpu_custom_call" | custom-call | tf_op jit(solution)/shard_map/pallas_call | solution.py:348
  61.7 3.6 %all-to-all-start.1 = ((f32[16,48,128]{2,1,0:T(8,128)}), f32[16,48,128]{2,1,0:T(8,128)S(1)}, u32[]{:S(2)}, u32[]{:S(2)}) async-start(f32[16,48,128]{2,1,0:T(8,128)} %shard_map.76), calls=%async_computation.1 | async-start | bytes 786432 | tf_op jit(solution)/shard_map/all_to_all | solution.py:358
  65.4 3.4 %shard_map.77 = (bf16[3072,256]{1,0:T(8,128)(2,1)S(1)}, f32[40,3072]{1,0:T(8,128)S(1)}) custom-call(f32[3,1024]{1,0:T(4,128)S(1)} %get-tuple-element.15.slot_ref, bf16[3072,256]{1,0:T(8,128)(2,1)S(1)} %copy-done, bf16[32,256]{1,0:T(8,128)(2,1)S(1)} %bitcast.26, f32[1,3072]{1,0:T(1,128)S(1)} %get-tuple-element.16.up_ref), custom_call_target="tpu_custom_call" | custom-call | tf_op jit(solution)/shard_map/pallas_call | solution.py:368
  68.8 1.2 %copy-done.1 = bf16[3072,256]{1,0:T(8,128)(2,1)} copy-done((bf16[3072,256]{1,0:T(8,128)(2,1)}, bf16[3072,256]{1,0:T(8,128)(2,1)S(1)}, u32[]{:S(2)}) %copy-start.1) | copy-done | bytes 1572888
  70.0 0.8 copy-done.3
  70.8 5.4 %all-to-all-done.1 = f32[16,48,128]{2,1,0:T(8,128)S(1)} async-done(((f32[16,48,128]{2,1,0:T(8,128)}), f32[16,48,128]{2,1,0:T(8,128)S(1)}, u32[]{:S(2)}, u32[]{:S(2)}) %all-to-all-start.1) | async-done | bytes 393248 | tf_op jit(solution)/shard_map/all_to_all | solution.py:358
  76.2 1.4 %copy-done.2 = bf16[3072,256]{1,0:T(8,128)(2,1)S(1)} copy-done((bf16[3072,256]{1,0:T(8,128)(2,1)S(1)}, bf16[3072,256]{1,0:T(8,128)(2,1)}, u32[]{:S(2)}) %copy-start.2) | copy-done | bytes 1572888
  77.6 1.4 %shard_map.78 = f32[32,256]{1,0:T(8,128)S(1)} custom-call(f32[768,128]{1,0:T(8,128)S(1)} %bitcast.21, bf16[3072,256]{1,0:T(8,128)(2,1)S(1)} %copy-done.2, f32[40,3072]{1,0:T(8,128)} %copy-done.3), custom_call_target="tpu_custom_call" | custom-call | tf_op jit(solution)/shard_map/pallas_call | solution.py:376
  79.1 0.1 collective-permute-start.8
  79.2 1.2 %collective-permute-done.8 = f32[48,128]{1,0:T(8,128)S(1)} collective-permute-done((f32[48,128]{1,0:T(8,128)S(1)}, f32[48,128]{1,0:T(8,128)S(1)}, u32[]{:S(2)}, u32[]{:S(2)}) %collective-permute-start.8) | collective-permute-done | bytes 24608 | tf_op jit(solution)/shard_map/ppermute | solution.py:383
  80.4 11.1 %all_to_all.20 = f32[8,48,128]{2,1,0:T(8,128)S(1)} all-to-all(f32[8,48,128]{2,1,0:T(8,128)S(1)} %broadcast_in_dim.10), channel_id=1, replica_groups={{0,16,32,48,64,80,96,112},{8,24,40,56,72,88,104,120},{1,17,33,49,65,81,..., dimensions={0} | all-to-all | bytes 393216 | tf_op jit(solution)/shard_map/all_to_all | solution.py:385
  91.5 11.6 %all_to_all.21 = f32[8,48,128]{2,1,0:T(8,128)S(1)} all-to-all(f32[8,48,128]{2,1,0:T(8,128)S(1)} %broadcast_in_dim.11), channel_id=1, replica_groups=mesh['walk'=16,'band'=8] {'band'}, dimensions={0} | all-to-all | bytes 393216 | tf_op jit(solution)/shard_map/all_to_all | solution.py:394
  103.1 0.1 reshape.40
  103.2 0.7 reshape.41
  (36 shorter events, 0.2 us)
Async XLA Ops:
  0.0 13.7 %copy-start.4 = (f32[2,3072]{1,0:T(2,128)S(1)}, f32[2,3072]{1,0:T(2,128)}, u32[]{:S(2)}) copy-start(f32[2,3072]{1,0:T(2,128)} %pos_ref) | copy-start | bytes 73732
  0.0 13.8 %copy-start.5 = (s32[3072]{0:T(1024)S(1)}, s32[3072]{0:T(1024)}, u32[]{:S(2)}) copy-start(s32[3072]{0:T(1024)} %param.10) | copy-start | bytes 36868
  0.0 15.9 %copy-start.6 = (s32[2,18432]{1,0:T(2,128)S(1)}, s32[2,18432]{1,0:T(2,128)}, u32[]{:S(2)}) copy-start(s32[2,18432]{1,0:T(2,128)} %param.9) | copy-start | bytes 442372
  2.6 40.1 %all-to-all-start = ((bf16[128,24,128]{2,1,0:T(8,128)(2,1)}), bf16[128,24,128]{2,1,0:T(8,128)(2,1)S(1)}, u32[]{:S(2)}, u32[]{:S(2)}) async-start(bf16[128,24,128]{2,1,0:T(8,128)(2,1)} %bitcast), calls=%async_computation | async-start | bytes 1572864 | tf_op jit(solution)/shard_map/all_to_all | solution.py:332
  15.8 1.2 %collective-permute-start = (f32[1,56,128]{2,1,0:T(8,128)S(1)}, f32[1,56,128]{2,1,0:T(8,128)S(1)}, u32[]{:S(2)}, u32[]{:S(2)}) collective-permute-start(f32[1,56,128]{2,1,0:T(8,128)S(1)} %bitcast.24), channel_id=1, source_target_pairs={{0,8},{8,0},{16,24},{24,16},{32,40},{40,32},{48,56},{56,48},{64,72... | collective-permute-start | bytes 86024 | tf_op jit(solution)/shard_map/ppermute | solution.py:343
  17.1 25.6 %collective-permute-start.7 = (f32[2,56,128]{2,1,0:T(8,128)S(1)}, f32[2,56,128]{2,1,0:T(8,128)S(1)}, u32[]{:S(2)}, u32[]{:S(2)}) collective-permute-start(f32[2,56,128]{2,1,0:T(8,128)S(1)} %pad_maximum_fusion), channel_id=1, source_target_pairs={{0,112},{8,120},{16,96},{24,104},{32,80},{40,88},{48,64},{56,72},{... | collective-permute-start | bytes 172040 | tf_op jit(solution)/shard_map/ppermute | solution.py:343
  22.4 20.2 %collective-permute-start.6 = (f32[2,56,128]{2,1,0:T(8,128)S(1)}, f32[2,56,128]{2,1,0:T(8,128)S(1)}, u32[]{:S(2)}, u32[]{:S(2)}) collective-permute-start(f32[2,56,128]{2,1,0:T(8,128)S(1)} %pad_maximum_fusion), channel_id=1, source_target_pairs={{0,96},{8,104},{16,112},{24,120},{32,64},{40,72},{48,80},{56,88},{... | collective-permute-start | bytes 172040 | tf_op jit(solution)/shard_map/ppermute | solution.py:343
  22.6 20.0 %collective-permute-start.5 = (f32[2,56,128]{2,1,0:T(8,128)S(1)}, f32[2,56,128]{2,1,0:T(8,128)S(1)}, u32[]{:S(2)}, u32[]{:S(2)}) collective-permute-start(f32[2,56,128]{2,1,0:T(8,128)S(1)} %pad_maximum_fusion), channel_id=1, source_target_pairs={{0,80},{8,88},{16,64},{24,72},{32,112},{40,120},{48,96},{56,104},{... | collective-permute-start | bytes 172040 | tf_op jit(solution)/shard_map/ppermute | solution.py:343
  25.5 17.1 %collective-permute-start.4 = (f32[2,56,128]{2,1,0:T(8,128)S(1)}, f32[2,56,128]{2,1,0:T(8,128)S(1)}, u32[]{:S(2)}, u32[]{:S(2)}) collective-permute-start(f32[2,56,128]{2,1,0:T(8,128)S(1)} %pad_maximum_fusion), channel_id=1, source_target_pairs={{0,64},{8,72},{16,80},{24,88},{32,96},{40,104},{48,112},{56,120},{... | collective-permute-start | bytes 172040 | tf_op jit(solution)/shard_map/ppermute | solution.py:343
  26.5 5.0 %collective-permute-start.1 = (f32[2,56,128]{2,1,0:T(8,128)S(1)}, f32[2,56,128]{2,1,0:T(8,128)S(1)}, u32[]{:S(2)}, u32[]{:S(2)}) collective-permute-start(f32[2,56,128]{2,1,0:T(8,128)S(1)} %pad_maximum_fusion), channel_id=1, source_target_pairs={{0,16},{8,24},{16,0},{24,8},{32,48},{40,56},{48,32},{56,40},{64,80... | collective-permute-start | bytes 172040 | tf_op jit(solution)/shard_map/ppermute | solution.py:343
  31.5 5.7 %collective-permute-start.2 = (f32[2,56,128]{2,1,0:T(8,128)S(1)}, f32[2,56,128]{2,1,0:T(8,128)S(1)}, u32[]{:S(2)}, u32[]{:S(2)}) collective-permute-start(f32[2,56,128]{2,1,0:T(8,128)S(1)} %pad_maximum_fusion), channel_id=1, source_target_pairs={{0,32},{8,40},{16,48},{24,56},{32,0},{40,8},{48,16},{56,24},{64,96... | collective-permute-start | bytes 172040 | tf_op jit(solution)/shard_map/ppermute | solution.py:343
  37.2 5.4 %collective-permute-start.3 = (f32[2,56,128]{2,1,0:T(8,128)S(1)}, f32[2,56,128]{2,1,0:T(8,128)S(1)}, u32[]{:S(2)}, u32[]{:S(2)}) collective-permute-start(f32[2,56,128]{2,1,0:T(8,128)S(1)} %pad_maximum_fusion), channel_id=1, source_target_pairs={{0,48},{8,56},{16,32},{24,40},{32,16},{40,24},{48,0},{56,8},{64,11... | collective-permute-start | bytes 172040 | tf_op jit(solution)/shard_map/ppermute | solution.py:343
  42.7 22.6 %copy-start.7 = (bf16[256,192]{0,1:T(8,128)(2,1)S(1)}, bf16[256,192]{0,1:T(8,128)(2,1)}, u32[]{:S(2)}) copy-start(bf16[256,192]{0,1:T(8,128)(2,1)} %param.13) | copy-start | bytes 294916
  42.7 22.7 %copy-start = (bf16[3072,256]{1,0:T(8,128)(2,1)S(1)}, bf16[3072,256]{1,0:T(8,128)(2,1)}, u32[]{:S(2)}) copy-start(bf16[3072,256]{1,0:T(8,128)(2,1)} %feature_ref.1) | copy-start | bytes 4718596
  61.7 14.6 %all-to-all-start.1 = ((f32[16,48,128]{2,1,0:T(8,128)}), f32[16,48,128]{2,1,0:T(8,128)S(1)}, u32[]{:S(2)}, u32[]{:S(2)}) async-start(f32[16,48,128]{2,1,0:T(8,128)} %shard_map.76), calls=%async_computation.1 | async-start | bytes 786432 | tf_op jit(solution)/shard_map/all_to_all | solution.py:358
  68.8 1.2 %copy-start.1 = (bf16[3072,256]{1,0:T(8,128)(2,1)}, bf16[3072,256]{1,0:T(8,128)(2,1)S(1)}, u32[]{:S(2)}) copy-start(bf16[3072,256]{1,0:T(8,128)(2,1)S(1)} %get-tuple-element.17.feature_ref) | copy-start | bytes 4718596
  70.0 0.8 copy-start.3
  76.2 1.4 %copy-start.2 = (bf16[3072,256]{1,0:T(8,128)(2,1)S(1)}, bf16[3072,256]{1,0:T(8,128)(2,1)}, u32[]{:S(2)}) copy-start(bf16[3072,256]{1,0:T(8,128)(2,1)} %copy-done.1) | copy-start | bytes 4718596
  79.1 1.3 %collective-permute-start.8 = (f32[48,128]{1,0:T(8,128)S(1)}, f32[48,128]{1,0:T(8,128)S(1)}, u32[]{:S(2)}, u32[]{:S(2)}) collective-permute-start(f32[48,128]{1,0:T(8,128)S(1)} %reshape.39), channel_id=1, source_target_pairs={{0,8},{8,0},{16,24},{24,16},{32,40},{40,32},{48,56},{56,48},{64,72... | collective-permute-start | bytes 73736 | tf_op jit(solution)/shard_map/ppermute | solution.py:383

commit v5 on v4

--- a/solution.py
+++ b/solution.py
@@ -200,7 +200,8 @@
     out_ref[...] = jnp.zeros_like(out_ref)
 
     def waves(group, length):
-        away = group ^ walk
+        flip = group ^ walk
+        away = ((groups - (flip & ~1)) & (groups - 1)) + (flip & 1)
         for line in range(0, 2 * chunks, 8):
             first = base_wave(pos_ref[away, line : line + 8, :])
             power = (jnp.ones((8, LANES), F32), jnp.zeros((8, LANES), F32))
@@ -339,7 +340,7 @@
         ),
     )(positions, spin_labels.reshape(chunks, LANES))
     everyone = ordered[None]
-    for flips in ((1,), tuple(range(2, walk_count, 2))):
+    for flips in ((1,), tuple(range(walk_count - 2, 0, -2))):
         moved = [lax.ppermute(everyone, "walk", [(k, k ^ flip) for k in range(walk_count)]) for flip in flips]
         everyone = jnp.concatenate([everyone, *moved], axis=0)
     table = call(

time: 104 us -> 109 us (1.048)
  waiting for transfers between devices: 17.5 us -> 25.8 us
  starting transfers between devices: 30.7 us -> 27.6 us
    ppermute x8, waiting for transfers between devices: 10.9 us -> 19.3 us  [local(): lax.ppermute(everyone, 'walk', [(k, k ^ flip) for k in range(walk_count)])]
    ppermute x8, starting transfers between devices: 15.8 us -> 11.8 us  [local(): lax.ppermute(everyone, 'walk', [(k, k ^ flip) for k in range(walk_count)])]
where the time goes in v5:
time: 109 us
  Pallas kernels  28.4 us (26%)
  starting transfers between devices  27.6 us (25%)
  waiting for transfers between devices  25.8 us (24%)
  blocking collectives  22.1 us (20%)
  local copies, waits for them, and re-layouts  4.35 us (4%)
    ppermute x8, waiting for transfers between devices, local(): lax.ppermute(everyone, 'walk', [(k, k ^ flip) for k in range(walk_count)])  19.3 us
    pallas_call x1, Pallas kernels, local(): call(functools.partial(orbital_kernel, unroll=12, each=each), jax.ShapeDt...  14.7 us
    ppermute x8, starting transfers between devices, local(): lax.ppermute(everyone, 'walk', [(k, k ^ flip) for k in range(walk_count)])  11.8 us
    all_to_all x1, starting transfers between devices, local(): lax.all_to_all(picked.reshape(devices, BLOCK, LANES), ('walk', 'band'), 0...  11.2 us
    all_to_all x1, blocking collectives, local(): lax.all_to_all(jnp.broadcast_to(own, (chips, *own.shape)), 'walk', 0, 0,...  11.1 us
    all_to_all x1, blocking collectives, local(): lax.all_to_all(jnp.broadcast_to(summed, (band_count, *own.shape)), 'band'...  11 us
    all_to_all x1, waiting for transfers between devices, local(): target = lax.all_to_all(values, 'walk', 0, 0, tiled=True).reshape(-1, LANES)  5.41 us
    all_to_all x1, starting transfers between devices, local(): target = lax.all_to_all(values, 'walk', 0, 0, tiled=True).reshape(-1, LANES)  4.62 us
  transfers between devices with their start and end apart: 11, of which 6 were waited for; matrix products, arithmetic and copies ran while one was open for 0% of the time, Pallas kernels for 5%

profile of v5, /device:TPU:0, one launch (start us, length us, event | category | flops | bytes accessed | tf_op | source)
XLA Modules:
  0.0 108.6 jit_solution(15625845015767704352)
XLA Ops:
  0.0 2.6 %shard_map.73 = bf16[3072,128]{1,0:T(8,128)(2,1)} custom-call(bf16[2,1152,128]{2,1,0:T(8,128)(2,1)} %coef_hbm.1, s32[2,48]{1,0:T(2,128)} %occ_hbm.1), custom_call_target="tpu_custom_call" | custom-call | tf_op jit(solution)/shard_map/pallas_call | solution.py:321
  2.6 11.2 %all-to-all-start = ((bf16[128,24,128]{2,1,0:T(8,128)(2,1)}), bf16[128,24,128]{2,1,0:T(8,128)(2,1)S(1)}, u32[]{:S(2)}, u32[]{:S(2)}) async-start(bf16[128,24,128]{2,1,0:T(8,128)(2,1)} %bitcast), calls=%async_computation | async-start | bytes 1572864 | tf_op jit(solution)/shard_map/all_to_all | solution.py:333
  13.8 2.1 %shard_map.75 = (f32[56,128]{1,0:T(8,128)S(1)}, f32[3,1024]{1,0:T(4,128)S(1)}, f32[1,3072]{1,0:T(1,128)S(1)}) custom-call(f32[2,3072]{1,0:T(2,128)S(1)} %copy-done.4, s32[24,128]{1,0:T(8,128)S(1)} %bitcast.27), custom_call_target="tpu_custom_call" | custom-call | tf_op jit(solution)/shard_map/pallas_call | solution.py:334
  15.9 1.2 %collective-permute-done = f32[1,56,128]{2,1,0:T(8,128)S(1)} collective-permute-done((f32[1,56,128]{2,1,0:T(8,128)S(1)}, f32[1,56,128]{2,1,0:T(8,128)S(1)}, u32[]{:S(2)}, u32[]{:S(2)}) %collective-permute-start) | collective-permute-done | bytes 28704 | tf_op jit(solution)/shard_map/ppermute | solution.py:344
  17.1 1.1 collective-permute-start.7
  18.1 3.2 %collective-permute-start.6 = (f32[2,56,128]{2,1,0:T(8,128)S(1)}, f32[2,56,128]{2,1,0:T(8,128)S(1)}, u32[]{:S(2)}, u32[]{:S(2)}) collective-permute-start(f32[2,56,128]{2,1,0:T(8,128)S(1)} %pad_maximum_fusion), channel_id=1, source_target_pairs={{0,32},{8,40},{16,48},{24,56},{32,0},{40,8},{48,16},{56,24},{64,96... | collective-permute-start | bytes 172040 | tf_op jit(solution)/shard_map/ppermute | solution.py:344
  21.4 0.4 collective-permute-start.5
  21.8 2.7 %collective-permute-start.4 = (f32[2,56,128]{2,1,0:T(8,128)S(1)}, f32[2,56,128]{2,1,0:T(8,128)S(1)}, u32[]{:S(2)}, u32[]{:S(2)}) collective-permute-start(f32[2,56,128]{2,1,0:T(8,128)S(1)} %pad_maximum_fusion), channel_id=1, source_target_pairs={{0,64},{8,72},{16,80},{24,88},{32,96},{40,104},{48,112},{56,120},{... | collective-permute-start | bytes 172040 | tf_op jit(solution)/shard_map/ppermute | solution.py:344
  24.5 3.1 %collective-permute-start.1 = (f32[2,56,128]{2,1,0:T(8,128)S(1)}, f32[2,56,128]{2,1,0:T(8,128)S(1)}, u32[]{:S(2)}, u32[]{:S(2)}) collective-permute-start(f32[2,56,128]{2,1,0:T(8,128)S(1)} %pad_maximum_fusion), channel_id=1, source_target_pairs={{0,112},{8,120},{16,96},{24,104},{32,80},{40,88},{48,64},{56,72},{... | collective-permute-start | bytes 172040 | tf_op jit(solution)/shard_map/ppermute | solution.py:344
  27.6 4.7 %collective-permute-done.1 = f32[2,56,128]{2,1,0:T(8,128)S(1)} collective-permute-done((f32[2,56,128]{2,1,0:T(8,128)S(1)}, f32[2,56,128]{2,1,0:T(8,128)S(1)}, u32[]{:S(2)}, u32[]{:S(2)}) %collective-permute-start.1) | collective-permute-done | bytes 57376 | tf_op jit(solution)/shard_map/ppermute | solution.py:344
  32.3 0.7 collective-permute-start.2
  33.0 7.4 %collective-permute-done.2 = f32[2,56,128]{2,1,0:T(8,128)S(1)} collective-permute-done((f32[2,56,128]{2,1,0:T(8,128)S(1)}, f32[2,56,128]{2,1,0:T(8,128)S(1)}, u32[]{:S(2)}, u32[]{:S(2)}) %collective-permute-start.2) | collective-permute-done | bytes 57376 | tf_op jit(solution)/shard_map/ppermute | solution.py:344
  40.3 0.6 collective-permute-start.3
  40.9 6.0 %collective-permute-done.3 = f32[2,56,128]{2,1,0:T(8,128)S(1)} collective-permute-done((f32[2,56,128]{2,1,0:T(8,128)S(1)}, f32[2,56,128]{2,1,0:T(8,128)S(1)}, u32[]{:S(2)}, u32[]{:S(2)}) %collective-permute-start.3) | collective-permute-done | bytes 57376 | tf_op jit(solution)/shard_map/ppermute | solution.py:344
  46.9 0.0 collective-permute-done.4
  47.0 0.0 copy-start.7
  47.1 0.0 copy-start
  47.1 4.2 %shard_map.74.table_ref = bf16[320,512]{1,0:T(8,128)(2,1)S(1)} custom-call(bf16[128,24,128]{2,1,0:T(8,128)(2,1)S(1)} %all-to-all-done.recv_ref, s32[2,16,1152]{2,1,0:T(8,128)S(1)} %bitcast.22), custom_call_target="tpu_custom_call" | custom-call | tf_op jit(solution)/shard_map/pallas_call | solution.py:346
  51.3 14.7 %shard_map.76 = f32[16,48,128]{2,1,0:T(8,128)} custom-call(bf16[320,512]{1,0:T(8,128)(2,1)S(1)} %shard_map.74.table_ref, f32[16,56,128]{2,1,0:T(8,128)S(1)} %constant_dynamic-update-slice_fusion.pos_ref), custom_call_target="tpu_custom_call" | custom-call | tf_op jit(solution)/shard_map/pallas_call | solution.py:349
  66.0 4.6 %all-to-all-start.1 = ((f32[16,48,128]{2,1,0:T(8,128)}), f32[16,48,128]{2,1,0:T(8,128)S(1)}, u32[]{:S(2)}, u32[]{:S(2)}) async-start(f32[16,48,128]{2,1,0:T(8,128)} %shard_map.76), calls=%async_computation.1 | async-start | bytes 786432 | tf_op jit(solution)/shard_map/all_to_all | solution.py:359
  70.8 3.4 %shard_map.77 = (bf16[3072,256]{1,0:T(8,128)(2,1)S(1)}, f32[40,3072]{1,0:T(8,128)S(1)}) custom-call(f32[3,1024]{1,0:T(4,128)S(1)} %get-tuple-element.15.slot_ref, bf16[3072,256]{1,0:T(8,128)(2,1)S(1)} %copy-done, bf16[32,256]{1,0:T(8,128)(2,1)S(1)} %bitcast.26, f32[1,3072]{1,0:T(1,128)S(1)} %get-tuple-element.16.up_ref), custom_call_target="tpu_custom_call" | custom-call | tf_op jit(solution)/shard_map/pallas_call | solution.py:369
  74.2 1.2 %copy-done.1 = bf16[3072,256]{1,0:T(8,128)(2,1)} copy-done((bf16[3072,256]{1,0:T(8,128)(2,1)}, bf16[3072,256]{1,0:T(8,128)(2,1)S(1)}, u32[]{:S(2)}) %copy-start.1) | copy-done | bytes 1572888
  75.3 0.8 copy-done.3
  76.2 5.4 %all-to-all-done.1 = f32[16,48,128]{2,1,0:T(8,128)S(1)} async-done(((f32[16,48,128]{2,1,0:T(8,128)}), f32[16,48,128]{2,1,0:T(8,128)S(1)}, u32[]{:S(2)}, u32[]{:S(2)}) %all-to-all-start.1) | async-done | bytes 393248 | tf_op jit(solution)/shard_map/all_to_all | solution.py:359
  81.6 1.4 %copy-done.2 = bf16[3072,256]{1,0:T(8,128)(2,1)S(1)} copy-done((bf16[3072,256]{1,0:T(8,128)(2,1)S(1)}, bf16[3072,256]{1,0:T(8,128)(2,1)}, u32[]{:S(2)}) %copy-start.2) | copy-done | bytes 1572888
  83.0 1.4 %shard_map.78 = f32[32,256]{1,0:T(8,128)S(1)} custom-call(f32[768,128]{1,0:T(8,128)S(1)} %bitcast.21, bf16[3072,256]{1,0:T(8,128)(2,1)S(1)} %copy-done.2, f32[40,3072]{1,0:T(8,128)} %copy-done.3), custom_call_target="tpu_custom_call" | custom-call | tf_op jit(solution)/shard_map/pallas_call | solution.py:377
  84.4 0.1 collective-permute-start.8
  84.5 1.2 %collective-permute-done.8 = f32[48,128]{1,0:T(8,128)S(1)} collective-permute-done((f32[48,128]{1,0:T(8,128)S(1)}, f32[48,128]{1,0:T(8,128)S(1)}, u32[]{:S(2)}, u32[]{:S(2)}) %collective-permute-start.8) | collective-permute-done | bytes 24608 | tf_op jit(solution)/shard_map/ppermute | solution.py:384
  85.7 11.1 %all_to_all.20 = f32[8,48,128]{2,1,0:T(8,128)S(1)} all-to-all(f32[8,48,128]{2,1,0:T(8,128)S(1)} %broadcast_in_dim.10), channel_id=1, replica_groups={{0,16,32,48,64,80,96,112},{8,24,40,56,72,88,104,120},{1,17,33,49,65,81,..., dimensions={0} | all-to-all | bytes 393216 | tf_op jit(solution)/shard_map/all_to_all | solution.py:386
  96.9 11.0 %all_to_all.21 = f32[8,48,128]{2,1,0:T(8,128)S(1)} all-to-all(f32[8,48,128]{2,1,0:T(8,128)S(1)} %broadcast_in_dim.11), channel_id=1, replica_groups=mesh['walk'=16,'band'=8] {'band'}, dimensions={0} | all-to-all | bytes 393216 | tf_op jit(solution)/shard_map/all_to_all | solution.py:395
  107.8 0.1 reshape.40
  107.9 0.7 reshape.41
  (36 shorter events, 0.2 us)
Async XLA Ops:
  0.0 13.7 %copy-start.4 = (f32[2,3072]{1,0:T(2,128)S(1)}, f32[2,3072]{1,0:T(2,128)}, u32[]{:S(2)}) copy-start(f32[2,3072]{1,0:T(2,128)} %pos_ref) | copy-start | bytes 73732
  0.0 13.8 %copy-start.5 = (s32[3072]{0:T(1024)S(1)}, s32[3072]{0:T(1024)}, u32[]{:S(2)}) copy-start(s32[3072]{0:T(1024)} %param.10) | copy-start | bytes 36868
  0.0 15.9 %copy-start.6 = (s32[2,18432]{1,0:T(2,128)S(1)}, s32[2,18432]{1,0:T(2,128)}, u32[]{:S(2)}) copy-start(s32[2,18432]{1,0:T(2,128)} %param.9) | copy-start | bytes 442372
  2.6 44.4 %all-to-all-start = ((bf16[128,24,128]{2,1,0:T(8,128)(2,1)}), bf16[128,24,128]{2,1,0:T(8,128)(2,1)S(1)}, u32[]{:S(2)}, u32[]{:S(2)}) async-start(bf16[128,24,128]{2,1,0:T(8,128)(2,1)} %bitcast), calls=%async_computation | async-start | bytes 1572864 | tf_op jit(solution)/shard_map/all_to_all | solution.py:333
  15.8 1.2 %collective-permute-start = (f32[1,56,128]{2,1,0:T(8,128)S(1)}, f32[1,56,128]{2,1,0:T(8,128)S(1)}, u32[]{:S(2)}, u32[]{:S(2)}) collective-permute-start(f32[1,56,128]{2,1,0:T(8,128)S(1)} %bitcast.24), channel_id=1, source_target_pairs={{0,8},{8,0},{16,24},{24,16},{32,40},{40,32},{48,56},{56,48},{64,72... | collective-permute-start | bytes 86024 | tf_op jit(solution)/shard_map/ppermute | solution.py:344
  17.1 29.9 %collective-permute-start.7 = (f32[2,56,128]{2,1,0:T(8,128)S(1)}, f32[2,56,128]{2,1,0:T(8,128)S(1)}, u32[]{:S(2)}, u32[]{:S(2)}) collective-permute-start(f32[2,56,128]{2,1,0:T(8,128)S(1)} %pad_maximum_fusion), channel_id=1, source_target_pairs={{0,16},{8,24},{16,0},{24,8},{32,48},{40,56},{48,32},{56,40},{64,80... | collective-permute-start | bytes 172040 | tf_op jit(solution)/shard_map/ppermute | solution.py:344
  18.1 28.8 %collective-permute-start.6 = (f32[2,56,128]{2,1,0:T(8,128)S(1)}, f32[2,56,128]{2,1,0:T(8,128)S(1)}, u32[]{:S(2)}, u32[]{:S(2)}) collective-permute-start(f32[2,56,128]{2,1,0:T(8,128)S(1)} %pad_maximum_fusion), channel_id=1, source_target_pairs={{0,32},{8,40},{16,48},{24,56},{32,0},{40,8},{48,16},{56,24},{64,96... | collective-permute-start | bytes 172040 | tf_op jit(solution)/shard_map/ppermute | solution.py:344
  21.4 25.6 %collective-permute-start.5 = (f32[2,56,128]{2,1,0:T(8,128)S(1)}, f32[2,56,128]{2,1,0:T(8,128)S(1)}, u32[]{:S(2)}, u32[]{:S(2)}) collective-permute-start(f32[2,56,128]{2,1,0:T(8,128)S(1)} %pad_maximum_fusion), channel_id=1, source_target_pairs={{0,48},{8,56},{16,32},{24,40},{32,16},{40,24},{48,0},{56,8},{64,11... | collective-permute-start | bytes 172040 | tf_op jit(solution)/shard_map/ppermute | solution.py:344
  21.8 25.2 %collective-permute-start.4 = (f32[2,56,128]{2,1,0:T(8,128)S(1)}, f32[2,56,128]{2,1,0:T(8,128)S(1)}, u32[]{:S(2)}, u32[]{:S(2)}) collective-permute-start(f32[2,56,128]{2,1,0:T(8,128)S(1)} %pad_maximum_fusion), channel_id=1, source_target_pairs={{0,64},{8,72},{16,80},{24,88},{32,96},{40,104},{48,112},{56,120},{... | collective-permute-start | bytes 172040 | tf_op jit(solution)/shard_map/ppermute | solution.py:344
  24.5 7.8 %collective-permute-start.1 = (f32[2,56,128]{2,1,0:T(8,128)S(1)}, f32[2,56,128]{2,1,0:T(8,128)S(1)}, u32[]{:S(2)}, u32[]{:S(2)}) collective-permute-start(f32[2,56,128]{2,1,0:T(8,128)S(1)} %pad_maximum_fusion), channel_id=1, source_target_pairs={{0,112},{8,120},{16,96},{24,104},{32,80},{40,88},{48,64},{56,72},{... | collective-permute-start | bytes 172040 | tf_op jit(solution)/shard_map/ppermute | solution.py:344
  32.3 8.1 %collective-permute-start.2 = (f32[2,56,128]{2,1,0:T(8,128)S(1)}, f32[2,56,128]{2,1,0:T(8,128)S(1)}, u32[]{:S(2)}, u32[]{:S(2)}) collective-permute-start(f32[2,56,128]{2,1,0:T(8,128)S(1)} %pad_maximum_fusion), channel_id=1, source_target_pairs={{0,96},{8,104},{16,112},{24,120},{32,64},{40,72},{48,80},{56,88},{... | collective-permute-start | bytes 172040 | tf_op jit(solution)/shard_map/ppermute | solution.py:344
  40.3 6.6 %collective-permute-start.3 = (f32[2,56,128]{2,1,0:T(8,128)S(1)}, f32[2,56,128]{2,1,0:T(8,128)S(1)}, u32[]{:S(2)}, u32[]{:S(2)}) collective-permute-start(f32[2,56,128]{2,1,0:T(8,128)S(1)} %pad_maximum_fusion), channel_id=1, source_target_pairs={{0,80},{8,88},{16,64},{24,72},{32,112},{40,120},{48,96},{56,104},{... | collective-permute-start | bytes 172040 | tf_op jit(solution)/shard_map/ppermute | solution.py:344
  47.0 23.6 %copy-start.7 = (bf16[256,192]{0,1:T(8,128)(2,1)S(1)}, bf16[256,192]{0,1:T(8,128)(2,1)}, u32[]{:S(2)}) copy-start(bf16[256,192]{0,1:T(8,128)(2,1)} %param.13) | copy-start | bytes 294916
  47.1 23.7 %copy-start = (bf16[3072,256]{1,0:T(8,128)(2,1)S(1)}, bf16[3072,256]{1,0:T(8,128)(2,1)}, u32[]{:S(2)}) copy-start(bf16[3072,256]{1,0:T(8,128)(2,1)} %feature_ref.1) | copy-start | bytes 4718596
  66.0 15.6 %all-to-all-start.1 = ((f32[16,48,128]{2,1,0:T(8,128)}), f32[16,48,128]{2,1,0:T(8,128)S(1)}, u32[]{:S(2)}, u32[]{:S(2)}) async-start(f32[16,48,128]{2,1,0:T(8,128)} %shard_map.76), calls=%async_computation.1 | async-start | bytes 786432 | tf_op jit(solution)/shard_map/all_to_all | solution.py:359
  74.2 1.2 %copy-start.1 = (bf16[3072,256]{1,0:T(8,128)(2,1)}, bf16[3072,256]{1,0:T(8,128)(2,1)S(1)}, u32[]{:S(2)}) copy-start(bf16[3072,256]{1,0:T(8,128)(2,1)S(1)} %get-tuple-element.17.feature_ref) | copy-start | bytes 4718596
  75.3 0.8 copy-start.3
  81.6 1.4 %copy-start.2 = (bf16[3072,256]{1,0:T(8,128)(2,1)S(1)}, bf16[3072,256]{1,0:T(8,128)(2,1)}, u32[]{:S(2)}) copy-start(bf16[3072,256]{1,0:T(8,128)(2,1)} %copy-done.1) | copy-start | bytes 4718596
  84.4 1.3 %collective-permute-start.8 = (f32[48,128]{1,0:T(8,128)S(1)}, f32[48,128]{1,0:T(8,128)S(1)}, u32[]{:S(2)}, u32[]{:S(2)}) collective-permute-start(f32[48,128]{1,0:T(8,128)S(1)} %reshape.39), channel_id=1, source_target_pairs={{0,8},{8,0},{16,24},{24,16},{32,40},{40,32},{48,56},{56,48},{64,72... | collective-permute-start | bytes 73736 | tf_op jit(solution)/shard_map/ppermute | solution.py:384
